TPU v7x, 32 devices: a whole 2x2x4 slice. The times are simulated.
32 devices in a mesh: pipe: 4 (over z), tensor: 4 (over x, core), dp: 2 (over y).
Axes of the slice: x: 2, y: 2, z: 4, core: 2. Of those that a mesh axis runs over, the one named last changes fastest.
Arguments:
- inputs: bfloat16 [2, 128, 4096], P(None, ('tensor', 'dp')), may hold values from -6 to 6
- weights: bfloat16 [2, 4, 4096, 4096], P(None, 'pipe', None, 'tensor'), may hold values from -0.09375 to 0.09375
- norm_gains: float32 [2, 4, 4096], P(None, 'pipe'), may hold values from 0.1 to 1.9
- cotangent: bfloat16 [2, 128, 4096], P(None, ('tensor', 'dp')), may hold values from -6 to 6
Outputs:
- act_factor: bfloat16 [4096, 2, 4, 4096], P(('tensor', 'dp'), None, 'pipe')
- grad_factor: bfloat16 [4096, 2, 4, 4096], P(('tensor', 'dp'), None, 'pipe')
All inputs are finite; a program needn't handle non-finite values.
Results may differ from a plain program's by a relative error of at most 0.025.
Values may be sent and summed in bfloat16 or wider, within the bound.
A program may use at most 192 MiB of HBM per device.

v0:
```python
import functools

import jax
import jax.numpy as jnp
from jax import lax
from jax.experimental import pallas as pl
from jax.experimental.pallas import tpu as pltpu
from jax.sharding import PartitionSpec as P

EPSILON = 1e-05


def peer_of(c, k):
    return lax.rem(c // 2 + k // 2, 2) * 2 + lax.rem(c + k, 2)


def chain_kernel(
    dims,
    x_ref,
    w_hbm,
    g_ref,
    cot_ref,
    h_out,
    d_out,
    w,
    hbuf,
    dcol,
    rms,
    acc,
    nxt,
    psend,
    rbuf,
    dnext,
    isend,
    irecv,
    w_sem,
    own_sem,
    in_send,
    in_recv,
    f1_send,
    f1_recv,
    fx_send,
    fx_recv,
    b1_send,
    b1_recv,
    rs_send,
    rs_recv,
    is_send,
    is_recv,
    dp_send,
    dp_recv,
    dg_send,
    dg_recv,
    loc_sem,
):
    micro, slots, rows, width, quarter, pipes, tensors, dps, cuts = dims
    items = slots * micro
    layers = slots * pipes
    group = tensors * rows
    part_rows = group // cuts
    p = lax.axis_index("pipe")
    c = lax.axis_index("tensor")
    d = lax.axis_index("dp")
    after = lax.rem(p + 1, pipes)
    before = lax.rem(p + pipes - 1, pipes)

    def where(pp, cc, dd):
        return {"pipe": pp, "tensor": cc, "dp": dd}

    def remote(src, dst, send, recv, target):
        return pltpu.make_async_remote_copy(
            src_ref=src,
            dst_ref=dst,
            send_sem=send,
            recv_sem=recv,
            device_id=target,
            device_id_type=pl.DeviceIdType.MESH,
        )

    w_copies = [
        pltpu.make_async_copy(w_hbm.at[s, 0], w.at[s], w_sem.at[s]) for s in range(slots)
    ]
    for copy in w_copies:
        copy.start()

    barrier = pltpu.get_barrier_semaphore()
    partners = [where(p, peer_of(c, k), d) for k in range(1, tensors)]
    partners += [where(after, c, d), where(before, c, d)]
    partners += [
        where(p, peer_of(c, k), lax.rem(d + e, dps)) for e in range(1, dps) for k in range(tensors)
    ]
    for partner in partners:
        pl.semaphore_signal(
            barrier, inc=1, device_id=partner, device_id_type=pl.DeviceIdType.MESH
        )
    pl.semaphore_wait(barrier, len(partners))

    def row_ds(cc):
        return pl.ds(pl.multiple_of(cc * rows, rows), rows)

    def col_ds(cc):
        return pl.ds(pl.multiple_of(cc * quarter, quarter), quarter)

    def opening(src, buf, m, k):
        whole = buf is hbuf
        return remote(
            src.at[m] if whole else src.at[m, :, col_ds(peer_of(c, k))],
            buf.at[m, row_ds(c)],
            in_send.at[m, k - 1],
            in_recv.at[m, k - 1],
            where(p, peer_of(c, k), d),
        )

    def opening_own(src, buf, m):
        whole = buf is hbuf
        return pltpu.make_async_copy(
            src.at[m] if whole else src.at[m, :, col_ds(c)], buf.at[m, row_ds(c)], own_sem.at[m]
        )

    def opening_all(src, buf):
        for m in range(micro):
            for k in range(1, tensors):
                opening(src, buf, m, k).start()
        for m in range(micro):
            opening_own(src, buf, m).start()

    def opening_wait(src, buf, m):
        opening_own(src, buf, m).wait()
        for k in range(1, tensors):
            opening(src, buf, m, k).wait_recv()

    @pl.when(p == 0)
    def _():
        opening_all(x_ref, hbuf)

    @pl.when(p == pipes - 1)
    def _():
        opening_all(cot_ref, dcol)

    def to_dp(item, slot, m, k):
        return remote(
            hbuf.at[item],
            h_out.at[slot, d, m],
            dp_send.at[item, k - 1],
            dp_recv.at[item, k - 1],
            where(p, c, lax.rem(d + k, dps)),
        )

    def to_own(item, slot, m):
        return pltpu.make_async_copy(hbuf.at[item], h_out.at[slot, d, m], loc_sem.at[0, item])

    def d_own(item, slot, m):
        return pltpu.make_async_copy(
            dcol.at[item], d_out.at[slot, d, m, :, col_ds(c)], loc_sem.at[1, item]
        )

    def d_share(item, slot, m, e, k):
        return remote(
            dcol.at[item],
            d_out.at[slot, d, m, :, col_ds(c)],
            dg_send.at[item, e, k],
            dg_recv.at[item, e, k],
            where(p, peer_of(c, k), lax.rem(d + e, dps)),
        )

    def d_shares(item, slot, m):
        return [
            d_share(item, slot, m, e, k)
            for e in range(dps - 1, -1, -1)
            for k in range(tensors - 1, -1, -1)
            if e or k
        ]

    def f_slice(item, cc, r):
        return hbuf.at[item, r * part_rows : (r + 1) * part_rows, col_ds(cc)]

    def f_along(item, target_item, r):
        return remote(
            nxt.at[item, r * part_rows : (r + 1) * part_rows],
            f_slice(target_item, c, r),
            f1_send.at[item, r],
            f1_recv.at[target_item, r],
            where(after, c, d),
        )

    def spread(item, part, r):
        owner = peer_of(c, 2) if part == 2 else c
        target = peer_of(c, 2) if part == 1 else peer_of(c, 1)
        ref = f_slice(item, owner, r)
        return remote(
            ref, ref, fx_send.at[item, part, r], fx_recv.at[item, part, r], where(p, target, d)
        )

    def f_step(item, carry):
        slot = item // micro
        m = lax.rem(item, micro)
        layer = slot * pipes + p
        target_item = item + micro * ((p + 1) // pipes)

        @pl.when(m == 0)
        def _():
            pltpu.make_async_copy(w_hbm.at[slot, 0], w.at[slot], w_sem.at[slot]).wait()

        @pl.when(layer == 0)
        def _():
            opening_wait(x_ref, hbuf, item)

        @pl.when(layer > 0)
        def _():
            for r in range(cuts):
                f_along(item, item, r).wait_recv()
                spread(item, 1, r).start()
                spread(item, 0, r).start()

        def piece(cc, first):
            part = hbuf[item, :, col_ds(cc)].astype(jnp.float32)
            scaled = (part * g_ref[slot, :, col_ds(cc)]).astype(jnp.bfloat16)
            product = jnp.dot(scaled, w[slot, col_ds(cc), :], preferred_element_type=jnp.float32)
            if first:
                acc[...] = product
            else:
                acc[...] += product
            return jnp.sum(part * part, axis=-1, keepdims=True)

        total = piece(c, True)

        @pl.when(layer > 0)
        def _():
            for r in range(cuts):
                spread(item, 0, r).wait_recv()

        total += piece(peer_of(c, 1), False)

        @pl.when(layer > 0)
        def _():
            for r in range(cuts):
                spread(item, 1, r).wait_recv()
                spread(item, 2, r).start()

        total += piece(peer_of(c, 2), False)

        @pl.when(layer > 0)
        def _():
            for r in range(cuts):
                spread(item, 2, r).wait_recv()

        total += piece(peer_of(c, 3), False)

        inverse_rms = lax.rsqrt(total * (1.0 / width) + EPSILON)
        rms[item] = jnp.broadcast_to(inverse_rms, (group, 128))

        @pl.when(layer < layers - 1)
        def _():
            product = (acc[...] * inverse_rms).astype(jnp.bfloat16).astype(jnp.float32)
            nxt[item] = (hbuf[item, :, col_ds(c)].astype(jnp.float32) + product).astype(
                jnp.bfloat16
            )
            for r in range(cuts):
                f_along(item, target_item, r).start()

        to_own(item, slot, m).start()
        for k in range(1, dps):
            to_dp(item, slot, m, k).start()
        return carry

    lax.fori_loop(0, items, f_step, 0)

    def b_along(item, target_item):
        return remote(
            dnext.at[item],
            dcol.at[target_item],
            b1_send.at[item],
            b1_recv.at[target_item],
            where(before, c, d),
        )

    def reduce_copy(item, k):
        return remote(
            psend.at[item, k],
            rbuf.at[item, k - 1],
            rs_send.at[item, k - 1],
            rs_recv.at[item, k - 1],
            where(p, peer_of(c, k), d),
        )

    def inner_copy(item, k):
        return remote(
            isend.at[item],
            irecv.at[item, k - 1],
            is_send.at[item, k - 1],
            is_recv.at[item, k - 1],
            where(p, peer_of(c, k), d),
        )

    def b_step(item, carry):
        slot = slots - 1 - item // micro
        m = lax.rem(item, micro)
        layer = slot * pipes + p
        target_item = item + micro * (1 - (p + pipes - 1) // pipes)
        stored = slot * micro + m

        @pl.when(layer == layers - 1)
        def _():
            opening_wait(cot_ref, dcol, item)

        @pl.when(layer < layers - 1)
        def _():
            b_along(item, item).wait_recv()

        @pl.when(layer == 0)
        def _():
            for share in d_shares(item, slot, m):
                share.start()

        d_own(item, slot, m).start()

        @pl.when(layer > 0)
        def _():
            columns = dcol[item]
            inner = jnp.zeros((group, 1), jnp.float32)
            for k in (3, 2, 1, 0):
                cc = peer_of(c, k)
                term = lax.dot_general(
                    columns,
                    w[slot, col_ds(cc), :],
                    (((1,), (1,)), ((), ())),
                    preferred_element_type=jnp.float32,
                ).astype(jnp.bfloat16)
                psend[item, k] = term
                if k:
                    reduce_copy(item, k).start()
                scaled = g_ref[slot, :, col_ds(cc)] * term.astype(jnp.float32)
                hidden = hbuf[stored, :, col_ds(cc)].astype(jnp.float32)
                inner += jnp.sum(hidden * scaled, axis=-1, keepdims=True)
            lanes = jnp.broadcast_to(inner, (group, 128))
            square = jnp.concatenate([lanes] * (128 // group), axis=0)
            isend[item] = jnp.transpose(square)[:8]
            for k in range(tensors - 1, 0, -1):
                inner_copy(item, k).start()

            for k in range(1, tensors):
                inner_copy(item, k).wait_recv()
            sums = isend[item]
            for k in range(1, tensors):
                sums += irecv[item, k - 1]
            inner_all = jnp.transpose(jnp.concatenate([sums] * 16, axis=0))[:group, :1]
            for k in (1, 2, 3):
                reduce_copy(item, k).wait_recv()
            back = psend[item, 0].astype(jnp.float32)
            for k in range(1, tensors):
                back += rbuf[item, k - 1].astype(jnp.float32)
            inverse_rms = rms[stored][:, :1]
            factor = inverse_rms * inverse_rms * inverse_rms * (inner_all * (1.0 / width))
            dnext[item] = (
                dcol[item].astype(jnp.float32)
                + inverse_rms * (g_ref[slot, :, col_ds(c)] * back)
                - factor * hbuf[stored, :, col_ds(c)].astype(jnp.float32)
            ).astype(jnp.bfloat16)
            b_along(item, target_item).start()

        @pl.when((layer > 0) & (m == micro - 1))
        def _():
            for q in range(micro):
                for share in d_shares(item - (micro - 1) + q, slot, q):
                    share.start()

        return carry

    lax.fori_loop(0, items, b_step, 0)

    @pl.when(p == 0)
    def _():
        for m in range(micro):
            for k in range(1, tensors):
                opening(x_ref, hbuf, m, k).wait_send()

    @pl.when(p == pipes - 1)
    def _():
        for m in range(micro):
            for k in range(1, tensors):
                opening(cot_ref, dcol, m, k).wait_send()

    def ending(item, carry):
        f_slot = item // micro
        b_slot = slots - 1 - item // micro
        m = lax.rem(item, micro)
        f_layer = f_slot * pipes + p
        b_layer = b_slot * pipes + p

        @pl.when(f_layer > 0)
        def _():
            for part in range(3):
                for r in range(cuts):
                    spread(item, part, r).wait_send()

        @pl.when(f_layer < layers - 1)
        def _():
            for r in range(cuts):
                f_along(item, item, r).wait_send()

        @pl.when(b_layer > 0)
        def _():
            b_along(item, item).wait_send()
            for k in range(1, tensors):
                reduce_copy(item, k).wait_send()
                inner_copy(item, k).wait_send()

        to_own(item, f_slot, m).wait()
        d_own(item, b_slot, m).wait()
        for k in range(1, dps):
            to_dp(item, f_slot, m, k).wait()
        for share in d_shares(item, b_slot, m):
            share.wait()
        return carry

    lax.fori_loop(0, items, ending, 0)


def chain(inputs, weights, norm_gains, cotangent):
    micro, rows, width = inputs.shape
    slots = weights.shape[0]
    quarter = weights.shape[3]
    pipes = lax.axis_size("pipe")
    tensors = lax.axis_size("tensor")
    dps = lax.axis_size("dp")
    items = slots * micro
    group = tensors * rows
    cuts = 4
    dims = (micro, slots, rows, width, quarter, pipes, tensors, dps, cuts)
    vmem = pl.BlockSpec(memory_space=pltpu.VMEM)
    hbm = pl.BlockSpec(memory_space=pl.ANY)
    dma = pltpu.SemaphoreType.DMA
    out = jax.ShapeDtypeStruct((slots, dps, micro, group, width), jnp.bfloat16)
    return pl.pallas_call(
        functools.partial(chain_kernel, dims),
        out_shape=(out, out),
        in_specs=[vmem, hbm, vmem, vmem],
        out_specs=(hbm, hbm),
        scratch_shapes=[
            pltpu.VMEM((slots, width, quarter), jnp.bfloat16),
            pltpu.VMEM((items, group, width), jnp.bfloat16),
            pltpu.VMEM((items, group, quarter), jnp.bfloat16),
            pltpu.VMEM((items, group, 128), jnp.float32),
            pltpu.VMEM((group, quarter), jnp.float32),
            pltpu.VMEM((items, group, quarter), jnp.bfloat16),
            pltpu.VMEM((items, tensors, group, quarter), jnp.bfloat16),
            pltpu.VMEM((items, tensors - 1, group, quarter), jnp.bfloat16),
            pltpu.VMEM((items, group, quarter), jnp.bfloat16),
            pltpu.VMEM((items, 8, 128), jnp.float32),
            pltpu.VMEM((items, tensors - 1, 8, 128), jnp.float32),
            dma((slots,)),
            dma((micro,)),
            dma((micro, tensors - 1)),
            dma((micro, tensors - 1)),
            dma((items, cuts)),
            dma((items, cuts)),
            dma((items, 3, cuts)),
            dma((items, 3, cuts)),
            dma((items,)),
            dma((items,)),
            dma((items, tensors - 1)),
            dma((items, tensors - 1)),
            dma((items, tensors - 1)),
            dma((items, tensors - 1)),
            dma((items, dps - 1)),
            dma((items, dps - 1)),
            dma((items, dps, tensors)),
            dma((items, dps, tensors)),
            dma((2, items)),
        ],
        compiler_params=pltpu.CompilerParams(
            collective_id=0, has_side_effects=True, vmem_limit_bytes=56 * 1024 * 1024
        ),
        name="chain",
    )(inputs, weights, norm_gains, cotangent)


def gram_kernel(base_rows, scale, normalized, x_ref, g_ref, out_ref, full, mixed):
    slots, tokens, width = x_ref.shape
    block = out_ref.shape[0]
    step = pl.program_id(0)

    if normalized:

        @pl.when(step == 0)
        def _():
            for s in range(slots):
                for t in range(0, tokens, 32):
                    wide = x_ref[s, t : t + 32].astype(jnp.float32)
                    mean = jnp.mean(wide * wide, axis=-1, keepdims=True)
                    inverse_rms = lax.rsqrt(mean + EPSILON)
                    full[s, t : t + 32] = (wide * inverse_rms * g_ref[s]).astype(jnp.bfloat16)

    source = full if normalized else x_ref
    own = (lax.axis_index("tensor") * lax.axis_size("dp") + lax.axis_index("dp")) * base_rows
    start = pl.multiple_of(own + step * block, block)
    columns = [source[s, :, pl.ds(start, block)] for s in range(slots)]
    span = 512
    for n in range(width // span):
        cut = slice(n * span, (n + 1) * span)
        for s in range(slots):
            gram = lax.dot_general(
                columns[s],
                source[s, :, cut],
                (((0,), (0,)), ((), ())),
                preferred_element_type=jnp.float32,
            )
            for q in range(span // 128):
                mixed[q, pl.ds(s, block, slots), :] = gram[:, q * 128 : (q + 1) * 128] * scale
        for q in range(span // 128):
            lane = slice(n * span + q * 128, n * span + (q + 1) * 128)
            out_ref[:, :, lane] = mixed[q].astype(jnp.bfloat16).reshape(block, slots, 128)


def gram_call(block, gains, own_rows, normalized):
    slots, tokens, width = block.shape
    tile = min(128, own_rows)
    out = pl.pallas_call(
        functools.partial(gram_kernel, own_rows, 1.0 / tokens, normalized),
        grid=(own_rows // tile,),
        out_shape=jax.ShapeDtypeStruct((own_rows, slots, width), jnp.bfloat16),
        in_specs=[
            pl.BlockSpec(block.shape, lambda i: (0, 0, 0), pipeline_mode=pl.Buffered(1)),
            pl.BlockSpec(gains.shape, lambda i: (0, 0, 0), pipeline_mode=pl.Buffered(1)),
        ],
        out_specs=pl.BlockSpec((tile, slots, width), lambda i: (i, 0, 0)),
        scratch_shapes=[
            pltpu.VMEM((slots, tokens, width) if normalized else (slots, 8, 128), jnp.bfloat16),
            pltpu.VMEM((4, tile * slots, 128), jnp.float32),
        ],
        compiler_params=pltpu.CompilerParams(vmem_limit_bytes=min(62 << 20, (32 << 20) + 8 * block.size)),
        name="gram",
    )(block, gains)
    return out.reshape(own_rows, slots, 1, width)


def body(inputs, weights, norm_gains, cotangent):
    micro, rows, width = inputs.shape
    slots = weights.shape[0]
    quarter = weights.shape[3]
    tensors = lax.axis_size("tensor")
    dps = lax.axis_size("dp")
    own_rows = quarter // dps
    tokens = micro * rows * tensors * dps
    h_all, d_all = chain(inputs, weights, norm_gains, cotangent)
    h_all = h_all.reshape(slots, tokens, width)
    d_all = d_all.reshape(slots, tokens, width)
    act = gram_call(h_all, norm_gains, own_rows, True)
    return act, gram_call(d_all, norm_gains, own_rows, False)


def solution(mesh):
    in_specs = (
        P(None, ("tensor", "dp"), None),
        P(None, "pipe", None, "tensor"),
        P(None, "pipe", None),
        P(None, ("tensor", "dp"), None),
    )
    out_specs = (P(("tensor", "dp"), None, "pipe", None), P(("tensor", "dp"), None, "pipe", None))
    return jax.shard_map(body, mesh=mesh, in_specs=in_specs, out_specs=out_specs, check_vma=False)
```

profile of v0, /device:TPU:1, one launch (start us, length us, event | category | flops | bytes accessed | tf_op | source)
XLA Modules:
  0.0 229.3 jit_solution(11105134186560096952)
XLA Ops:
  0.6 0.0 copy-start.2
  0.6 204.0 %chain.1 = (bf16[2,2,2,64,4096]{4,3,2,1,0:T(8,128)(2,1)}, bf16[2,2,2,64,4096]{4,3,2,1,0:T(8,128)(2,1)}) custom-call(bf16[2,16,4096]{2,1,0:T(8,128)(2,1)} %x_ref.1, bf16[2,1,4096,1024]{3,2,1,0:T(8,128)(2,1)} %w_hbm.1, f32[2,1,4096]{2,1,0:T(1,128)} %g_ref.5, bf16[2,16,4096]{2,1,0:T(8,128)(2,1)} %cot_ref.1), custom_call_target="tpu_custom_call" | custom-call | tf_op jit(solution)/shard_map/chain/pallas_call | solution.py:434
  204.6 0.0 copy-start
  204.7 0.0 copy-done.2
  204.7 0.0 copy-start.1
  204.7 2.3 %copy-done.1 = bf16[2,2,2,64,4096]{4,3,2,1,0:T(8,128)(2,1)S(1)} copy-done((bf16[2,2,2,64,4096]{4,3,2,1,0:T(8,128)(2,1)S(1)}, bf16[2,2,2,64,4096]{4,3,2,1,0:T(8,128)(2,1)}, u32[]{:S(2)}) %copy-start.1) | copy-done | bytes 4194328
  207.0 10.0 %gram.3 = bf16[512,2,4096]{2,1,0:T(2,128)(2,1)} custom-call(bf16[2,256,4096]{2,1,0:T(8,128)(2,1)S(1)} %bitcast.9, f32[2,1,4096]{2,1,0:T(1,128)S(1)} %copy-done.2), custom_call_target="tpu_custom_call" | custom-call | tf_op jit(solution)/shard_map/gram/pallas_call | solution.py:518
  217.0 0.0 copy-done
  217.0 12.3 %gram.2 = bf16[512,2,4096]{2,1,0:T(2,128)(2,1)} custom-call(bf16[2,256,4096]{2,1,0:T(8,128)(2,1)S(1)} %bitcast.8, f32[2,1,4096]{2,1,0:T(1,128)S(1)} %copy-done.2), custom_call_target="tpu_custom_call" | custom-call | tf_op jit(solution)/shard_map/gram/pallas_call | solution.py:518
Async XLA Ops:
  0.6 204.0 %copy-start.2 = (f32[2,1,4096]{2,1,0:T(1,128)S(1)}, f32[2,1,4096]{2,1,0:T(1,128)}, u32[]{:S(2)}) copy-start(f32[2,1,4096]{2,1,0:T(1,128)} %g_ref.5) | copy-start | bytes 98308
  204.6 12.4 %copy-start = (bf16[2,2,2,64,4096]{4,3,2,1,0:T(8,128)(2,1)S(1)}, bf16[2,2,2,64,4096]{4,3,2,1,0:T(8,128)(2,1)}, u32[]{:S(2)}) copy-start(bf16[2,2,2,64,4096]{4,3,2,1,0:T(8,128)(2,1)} %get-tuple-element.4) | copy-start | bytes 12582916
  204.7 2.3 %copy-start.1 = (bf16[2,2,2,64,4096]{4,3,2,1,0:T(8,128)(2,1)S(1)}, bf16[2,2,2,64,4096]{4,3,2,1,0:T(8,128)(2,1)}, u32[]{:S(2)}) copy-start(bf16[2,2,2,64,4096]{4,3,2,1,0:T(8,128)(2,1)} %get-tuple-element.5) | copy-start | bytes 12582916
where the time goes:
time: 234 us; the launch traced here: 229 us
  Pallas kernels  226 us (97%)
  local copies, waits for them, and re-layouts  2.34 us (1%)
    pallas_call x1, Pallas kernels, chain(): pl.pallas_call(functools.partial(chain_kernel, dims), out_shape=(out, out...  204 us
    pallas_call x2, Pallas kernels, gram_call(): pl.pallas_call(functools.partial(gram_kernel, own_rows, 1.0 / tokens, nor...  22.3 us

commit v1 on v0

v1 whole, which is shorter than its diff:
```python
import functools

import jax
import jax.numpy as jnp
from jax import lax
from jax.experimental import pallas as pl
from jax.experimental.pallas import tpu as pltpu
from jax.sharding import PartitionSpec as P

EPSILON = 1e-05
SPLITS = 2
CUTS = 2


def peer_of(c, k):
    return lax.rem(c // 2 + k // 2, 2) * 2 + lax.rem(c + k, 2)


def chain_kernel(
    dims,
    x_ref,
    w_hbm,
    g_ref,
    cot_ref,
    h_out,
    d_out,
    w,
    hbuf,
    dcol,
    rms,
    acc,
    nxt,
    own,
    far_send,
    far_recv,
    near_send,
    near_recv,
    x_send,
    x_recv,
    dnext,
    isend,
    irecv,
    w_sem,
    own_sem,
    in_send,
    in_recv,
    f1_send,
    f1_recv,
    fx_send,
    fx_recv,
    b1_send,
    b1_recv,
    s3_send,
    s3_recv,
    s1_send,
    s1_recv,
    xc_send,
    xc_recv,
    is_send,
    is_recv,
    dp_send,
    dp_recv,
    dg_send,
    dg_recv,
    loc_sem,
):
    chunks, splits, slots, rows, width, quarter, pipes, tensors, dps, cuts = dims
    items = slots * chunks
    layers = slots * pipes
    group = tensors * rows
    cut = quarter // cuts
    p = lax.axis_index("pipe")
    c = lax.axis_index("tensor")
    d = lax.axis_index("dp")
    after = lax.rem(p + 1, pipes)
    before = lax.rem(p + pipes - 1, pipes)

    def where(pp, cc, dd):
        return {"pipe": pp, "tensor": cc, "dp": dd}

    def remote(src, dst, send, recv, target):
        return pltpu.make_async_remote_copy(
            src_ref=src,
            dst_ref=dst,
            send_sem=send,
            recv_sem=recv,
            device_id=target,
            device_id_type=pl.DeviceIdType.MESH,
        )

    def w_copy(s):
        return pltpu.make_async_copy(w_hbm.at[s, 0], w.at[s], w_sem.at[s])

    for s in range(slots):
        w_copy(s).start()

    barrier = pltpu.get_barrier_semaphore()
    partners = [where(p, peer_of(c, k), d) for k in range(1, tensors)]
    partners += [where(after, c, d), where(before, c, d)]
    partners += [
        where(p, peer_of(c, k), lax.rem(d + e, dps)) for e in range(1, dps) for k in range(tensors)
    ]
    for partner in partners:
        pl.semaphore_signal(
            barrier, inc=1, device_id=partner, device_id_type=pl.DeviceIdType.MESH
        )
    pl.semaphore_wait(barrier, len(partners))

    def row_ds(cc):
        return pl.ds(pl.multiple_of(cc * rows, rows), rows)

    def col_ds(cc):
        return pl.ds(pl.multiple_of(cc * quarter, quarter), quarter)

    def cut_ds(cc, r):
        return pl.ds(pl.multiple_of(cc * quarter + r * cut, cut), cut)

    def span(r):
        return slice(r * cut, (r + 1) * cut)

    def opening_src(src, buf, q, cc):
        m, t = q // splits, q % splits
        part = src.at[m, t * rows : (t + 1) * rows]
        return part if buf is hbuf else part.at[:, col_ds(cc)]

    def opening(src, buf, q, k):
        return remote(
            opening_src(src, buf, q, peer_of(c, k)),
            buf.at[q, row_ds(c)],
            in_send.at[q, k - 1],
            in_recv.at[q, k - 1],
            where(p, peer_of(c, k), d),
        )

    def opening_own(src, buf, q):
        return pltpu.make_async_copy(
            opening_src(src, buf, q, c), buf.at[q, row_ds(c)], own_sem.at[q]
        )

    def opening_all(src, buf):
        for q in range(chunks):
            for k in (2, 3, 1):
                opening(src, buf, q, k).start()
        for q in range(chunks):
            opening_own(src, buf, q).start()

    def opening_wait(src, buf, q):
        whole = src.at[0, 0:rows]
        for k in range(1, tensors):
            part = whole if buf is hbuf else whole.at[:, col_ds(c)]
            remote(
                part,
                buf.at[q, row_ds(c)],
                in_send.at[q, k - 1],
                in_recv.at[q, k - 1],
                where(p, peer_of(c, k), d),
            ).wait_recv()
        part = whole if buf is hbuf else whole.at[:, col_ds(c)]
        pltpu.make_async_copy(part, buf.at[q, row_ds(c)], own_sem.at[q]).wait()

    @pl.when(p == 0)
    def _():
        opening_all(x_ref, hbuf)

    @pl.when(p == pipes - 1)
    def _():
        opening_all(cot_ref, dcol)

    def to_dp(item, slot, q, k):
        return remote(
            hbuf.at[item],
            h_out.at[slot, d, q],
            dp_send.at[item, k - 1],
            dp_recv.at[item, k - 1],
            where(p, c, lax.rem(d + k, dps)),
        )

    def to_own(item, slot, q):
        return pltpu.make_async_copy(hbuf.at[item], h_out.at[slot, d, q], loc_sem.at[0, item])

    def h_shares(item, slot, q):
        to_own(item, slot, q).start()
        for k in range(1, dps):
            to_dp(item, slot, q, k).start()

    def d_own(item, slot, q):
        return pltpu.make_async_copy(
            dcol.at[item], d_out.at[slot, d, q, :, col_ds(c)], loc_sem.at[1, item]
        )

    def d_share(item, slot, q, e, k):
        return remote(
            dcol.at[item],
            d_out.at[slot, d, q, :, col_ds(c)],
            dg_send.at[item, e, k],
            dg_recv.at[item, e, k],
            where(p, peer_of(c, k), lax.rem(d + e, dps)),
        )

    def d_shares(item, slot, q):
        return [
            d_share(item, slot, q, e, k)
            for e in range(dps - 1, -1, -1)
            for k in range(tensors - 1, -1, -1)
            if e or k
        ]

    def f_along(item, target_item, r):
        return remote(
            nxt.at[item, :, span(r)],
            hbuf.at[target_item, :, cut_ds(c, r)],
            f1_send.at[item, r],
            f1_recv.at[target_item, r],
            where(after, c, d),
        )

    def spread(item, part, r):
        owner = peer_of(c, 2) if part == 2 else c
        target = peer_of(c, 2) if part == 1 else peer_of(c, 1)
        ref = hbuf.at[item, :, cut_ds(owner, r)]
        return remote(
            ref, ref, fx_send.at[item, part, r], fx_recv.at[item, part, r], where(p, target, d)
        )

    def b_along(item, target_item, r):
        return remote(
            dnext.at[item, :, span(r)],
            dcol.at[target_item, :, span(r)],
            b1_send.at[item, r],
            b1_recv.at[target_item, r],
            where(before, c, d),
        )

    def far_copy(item, r):
        return remote(
            far_send.at[item, :, span(r)],
            far_recv.at[item, :, span(r)],
            s3_send.at[item, r],
            s3_recv.at[item, r],
            where(p, peer_of(c, 1), d),
        )

    def near_copy(item, r):
        return remote(
            near_send.at[item, :, span(r)],
            near_recv.at[item, :, span(r)],
            s1_send.at[item, r],
            s1_recv.at[item, r],
            where(p, peer_of(c, 1), d),
        )

    def x_copy(item, r):
        return remote(
            x_send.at[item, :, span(r)],
            x_recv.at[item, :, span(r)],
            xc_send.at[item, r],
            xc_recv.at[item, r],
            where(p, peer_of(c, 2), d),
        )

    def inner_copy(item, k):
        return remote(
            isend.at[item],
            irecv.at[item, k - 1],
            is_send.at[item, k - 1],
            is_recv.at[item, k - 1],
            where(p, peer_of(c, k), d),
        )

    def sums_start(item, first, second):
        lanes = [jnp.broadcast_to(v, (group, 128)) for v in (first, second)]
        square = jnp.concatenate([lanes[i % 2] for i in range(128 // group)], axis=0)
        isend[item] = jnp.transpose(square)[:8]
        for k in range(tensors - 1, 0, -1):
            inner_copy(item, k).start()

    def sums_finish(item):
        for k in range(1, tensors):
            inner_copy(item, k).wait_recv()
        sums = isend[item]
        for k in range(1, tensors):
            sums += irecv[item, k - 1]
        upright = jnp.transpose(jnp.concatenate([sums] * 16, axis=0))
        return upright[:group, :1], upright[group : 2 * group, :1]

    def reduce(item, slot, stored):
        columns = dcol[item]
        inner = jnp.zeros((group, 1), jnp.float32)
        order = [(3, r) for r in range(cuts)] + [(1, 0)] + [(2, r) for r in range(cuts)]
        order += [(1, r) for r in range(1, cuts)] + [(0, r) for r in range(cuts)]
        for k, r in order:
            where_to = cut_ds(peer_of(c, k), r)
            term = lax.dot_general(
                columns,
                w[slot, where_to, :],
                (((1,), (1,)), ((), ())),
                preferred_element_type=jnp.float32,
            ).astype(jnp.bfloat16)
            if k == 3:
                far_send[item, :, span(r)] = term
                far_copy(item, r).start()
            elif k == 2:
                far_copy(item, r).wait_recv()
                x_send[item, :, span(r)] = (
                    term.astype(jnp.float32) + far_recv[item, :, span(r)].astype(jnp.float32)
                ).astype(jnp.bfloat16)
                x_copy(item, r).start()
            elif k == 1:
                near_send[item, :, span(r)] = term
                near_copy(item, r).start()
            else:
                own[item, :, span(r)] = term
            if stored is not None:
                scaled = g_ref[slot, :, where_to] * term.astype(jnp.float32)
                hidden = hbuf[stored, :, where_to].astype(jnp.float32)
                inner += jnp.sum(hidden * scaled, axis=-1, keepdims=True)
        return inner

    def reduce_wait(item, r):
        near_copy(item, r).wait_recv()
        x_copy(item, r).wait_recv()

    def back_of(item, r):
        return (
            own[item, :, span(r)].astype(jnp.float32)
            + near_recv[item, :, span(r)].astype(jnp.float32)
            + x_recv[item, :, span(r)].astype(jnp.float32)
        )

    def finalize(item, slot, stored, inner_all, inverse_rms, waiting):
        factor = inverse_rms * inverse_rms * inverse_rms * (inner_all * (1.0 / width))
        target_item = item + chunks * (1 - (p + pipes - 1) // pipes)
        for r in range(cuts):
            if waiting:
                reduce_wait(item, r)
            dnext[item, :, span(r)] = (
                dcol[item, :, span(r)].astype(jnp.float32)
                + inverse_rms * (g_ref[slot, :, cut_ds(c, r)] * back_of(item, r))
                - factor * hbuf[stored, :, cut_ds(c, r)].astype(jnp.float32)
            ).astype(jnp.bfloat16)
            b_along(item, target_item, r).start()

    def turn_ahead(q, carry):
        opening_wait(cot_ref, dcol, q)
        d_own(q, slots - 1, q).start()
        reduce(q, slots - 1, None)
        for r in range(cuts):
            reduce_wait(q, r)
        return carry

    def turn_after(q, carry):
        item = (slots - 1) * chunks + q
        for r in range(cuts):
            spread(item, 1, r).wait_recv()
            spread(item, 2, r).start()
        for r in range(cuts):
            spread(item, 0, r).wait_recv()
            spread(item, 2, r).wait_recv()
        h_shares(item, slots - 1, q)
        for share in d_shares(q, slots - 1, q):
            share.start()
        return carry

    def f_step(item, carry):
        slot = item // chunks
        q = lax.rem(item, chunks)
        layer = slot * pipes + p
        target_item = item + chunks * ((p + 1) // pipes)

        @pl.when((layer == layers - 1) & (q == 0))
        def _():
            w_copy(slots - 1).wait()
            lax.fori_loop(0, chunks, turn_ahead, 0)

        @pl.when((layer < layers - 1) & (q == 0))
        def _():
            w_copy(slot).wait()

        @pl.when(layer == 0)
        def _():
            opening_wait(x_ref, hbuf, item)

        @pl.when(layer > 0)
        def _():
            for r in range(cuts):
                f_along(item, item, r).wait_recv()
                spread(item, 1, r).start()
                spread(item, 0, r).start()

        @pl.when(layer < layers - 1)
        def _():
            def scaled_of(cc, r):
                part = hbuf[item, :, cut_ds(cc, r)].astype(jnp.float32)
                scaled = (part * g_ref[slot, :, cut_ds(cc, r)]).astype(jnp.bfloat16)
                return scaled, jnp.sum(part * part, axis=-1, keepdims=True)

            def piece(cc, r, first=False):
                scaled, square = scaled_of(cc, r)
                product = jnp.dot(
                    scaled, w[slot, cut_ds(cc, r), :], preferred_element_type=jnp.float32
                )
                if first:
                    acc[...] = product
                else:
                    acc[...] += product
                return square

            total = piece(c, 0, True)
            for r in range(1, cuts):
                total += piece(c, r)

            @pl.when(layer > 0)
            def _():
                for r in range(cuts):
                    spread(item, 0, r).wait_recv()

            for r in range(cuts):
                total += piece(peer_of(c, 1), r)

            for r in range(cuts):

                @pl.when(layer > 0)
                def _(r=r):
                    spread(item, 1, r).wait_recv()
                    spread(item, 2, r).start()

                total += piece(peer_of(c, 2), r)

            for r in range(cuts):

                @pl.when(layer > 0)
                def _(r=r):
                    spread(item, 2, r).wait_recv()

                if r < cuts - 1:
                    total += piece(peer_of(c, 3), r)

            last = cut_ds(peer_of(c, 3), cuts - 1)
            scaled, square = scaled_of(peer_of(c, 3), cuts - 1)
            inverse_rms = lax.rsqrt((total + square) * (1.0 / width) + EPSILON)
            for n in range(cuts):
                product = acc[:, span(n)] + jnp.dot(
                    scaled, w[slot, last, span(n)], preferred_element_type=jnp.float32
                )
                product = (product * inverse_rms).astype(jnp.bfloat16).astype(jnp.float32)
                nxt[item, :, span(n)] = (
                    hbuf[item, :, cut_ds(c, n)].astype(jnp.float32) + product
                ).astype(jnp.bfloat16)
                f_along(item, target_item, n).start()
            rms[item] = jnp.broadcast_to(inverse_rms, (group, 128))
            h_shares(item, slot, q)

        @pl.when(layer == layers - 1)
        def _():
            inner = jnp.zeros((group, 1), jnp.float32)
            square = jnp.zeros((group, 1), jnp.float32)
            for r in range(cuts):
                hidden = hbuf[item, :, cut_ds(c, r)].astype(jnp.float32)
                scaled = g_ref[slot, :, cut_ds(c, r)] * back_of(q, r)
                inner += jnp.sum(hidden * scaled, axis=-1, keepdims=True)
                square += jnp.sum(hidden * hidden, axis=-1, keepdims=True)
            sums_start(q, inner, square)
            inner_all, square_all = sums_finish(q)
            inverse_rms = lax.rsqrt(square_all * (1.0 / width) + EPSILON)
            finalize(q, slot, item, inner_all, inverse_rms, False)

        @pl.when((layer == layers - 1) & (q == chunks - 1))
        def _():
            lax.fori_loop(0, chunks, turn_after, 0)

        return carry

    lax.fori_loop(0, items, f_step, 0)

    def b_step(item, carry):
        slot = slots - 1 - item // chunks
        q = lax.rem(item, chunks)
        layer = slot * pipes + p
        stored = slot * chunks + q

        @pl.when(layer < layers - 1)
        def _():
            for r in range(cuts):
                b_along(item, item, r).wait_recv()

        @pl.when(layer == 0)
        def _():
            for share in d_shares(item, slot, q):
                share.start()

        @pl.when(layer < layers - 1)
        def _():
            d_own(item, slot, q).start()

        @pl.when((layer > 0) & (layer < layers - 1))
        def _():
            inner = reduce(item, slot, stored)
            sums_start(item, inner, inner)
            inner_all, _ = sums_finish(item)
            finalize(item, slot, stored, inner_all, rms[stored][:, :1], True)

        @pl.when((layer > 0) & (layer < layers - 1) & (q == chunks - 1))
        def _():
            for back in range(chunks):
                for share in d_shares(item - (chunks - 1) + back, slot, back):
                    share.start()

        return carry

    lax.fori_loop(0, items, b_step, 0)

    @pl.when(p == 0)
    def _():
        for q in range(chunks):
            for k in range(1, tensors):
                opening(x_ref, hbuf, q, k).wait_send()

    @pl.when(p == pipes - 1)
    def _():
        for q in range(chunks):
            for k in range(1, tensors):
                opening(cot_ref, dcol, q, k).wait_send()

    def ending(item, carry):
        f_slot = item // chunks
        b_slot = slots - 1 - item // chunks
        q = lax.rem(item, chunks)
        f_layer = f_slot * pipes + p
        b_layer = b_slot * pipes + p

        @pl.when(f_layer > 0)
        def _():
            for part in range(3):
                for r in range(cuts):
                    spread(item, part, r).wait_send()

        @pl.when(f_layer < layers - 1)
        def _():
            for r in range(cuts):
                f_along(item, item, r).wait_send()

        @pl.when(b_layer > 0)
        def _():
            for r in range(cuts):
                b_along(item, item, r).wait_send()
                far_copy(item, r).wait_send()
                near_copy(item, r).wait_send()
                x_copy(item, r).wait_send()
            for k in range(1, tensors):
                inner_copy(item, k).wait_send()

        to_own(item, f_slot, q).wait()
        d_own(item, b_slot, q).wait()
        for k in range(1, dps):
            to_dp(item, f_slot, q, k).wait()
        for share in d_shares(item, b_slot, q):
            share.wait()
        return carry

    lax.fori_loop(0, items, ending, 0)


def chain(inputs, weights, norm_gains, cotangent):
    micro, own_rows, width = inputs.shape
    slots = weights.shape[0]
    quarter = weights.shape[3]
    pipes = lax.axis_size("pipe")
    tensors = lax.axis_size("tensor")
    dps = lax.axis_size("dp")
    splits = SPLITS
    cuts = CUTS
    rows = own_rows // splits
    chunks = micro * splits
    items = slots * chunks
    group = tensors * rows
    dims = (chunks, splits, slots, rows, width, quarter, pipes, tensors, dps, cuts)
    vmem = pl.BlockSpec(memory_space=pltpu.VMEM)
    hbm = pl.BlockSpec(memory_space=pl.ANY)
    dma = pltpu.SemaphoreType.DMA
    out = jax.ShapeDtypeStruct((slots, dps, chunks, group, width), jnp.bfloat16)
    piece = pltpu.VMEM((items, group, quarter), jnp.bfloat16)
    return pl.pallas_call(
        functools.partial(chain_kernel, dims),
        out_shape=(out, out),
        in_specs=[vmem, hbm, vmem, vmem],
        out_specs=(hbm, hbm),
        scratch_shapes=[
            pltpu.VMEM((slots, width, quarter), jnp.bfloat16),
            pltpu.VMEM((items, group, width), jnp.bfloat16),
            piece,
            pltpu.VMEM((items, group, 128), jnp.float32),
            pltpu.VMEM((group, quarter), jnp.float32),
            piece,
            piece,
            piece,
            piece,
            piece,
            piece,
            piece,
            piece,
            piece,
            pltpu.VMEM((items, 8, 128), jnp.float32),
            pltpu.VMEM((items, tensors - 1, 8, 128), jnp.float32),
            dma((slots,)),
            dma((chunks,)),
            dma((chunks, tensors - 1)),
            dma((chunks, tensors - 1)),
            dma((items, cuts)),
            dma((items, cuts)),
            dma((items, 3, cuts)),
            dma((items, 3, cuts)),
            dma((items, cuts)),
            dma((items, cuts)),
            dma((items, cuts)),
            dma((items, cuts)),
            dma((items, cuts)),
            dma((items, cuts)),
            dma((items, cuts)),
            dma((items, cuts)),
            dma((items, tensors - 1)),
            dma((items, tensors - 1)),
            dma((items, dps - 1)),
            dma((items, dps - 1)),
            dma((items, dps, tensors)),
            dma((items, dps, tensors)),
            dma((2, items)),
        ],
        compiler_params=pltpu.CompilerParams(
            collective_id=0, has_side_effects=True, vmem_limit_bytes=56 * 1024 * 1024
        ),
        name="chain",
    )(inputs, weights, norm_gains, cotangent)


def gram_kernel(base_rows, scale, normalized, x_ref, g_ref, out_ref, full, mixed):
    slots, tokens, width = x_ref.shape
    block = out_ref.shape[0]
    step = pl.program_id(0)

    if normalized:

        @pl.when(step == 0)
        def _():
            for s in range(slots):
                for t in range(0, tokens, 32):
                    wide = x_ref[s, t : t + 32].astype(jnp.float32)
                    mean = jnp.mean(wide * wide, axis=-1, keepdims=True)
                    inverse_rms = lax.rsqrt(mean + EPSILON)
                    full[s, t : t + 32] = (wide * inverse_rms * g_ref[s]).astype(jnp.bfloat16)

    source = full if normalized else x_ref
    own = (lax.axis_index("tensor") * lax.axis_size("dp") + lax.axis_index("dp")) * base_rows
    start = pl.multiple_of(own + step * block, block)
    columns = [source[s, :, pl.ds(start, block)] for s in range(slots)]
    span = 512
    for n in range(width // span):
        cut = slice(n * span, (n + 1) * span)
        for s in range(slots):
            gram = lax.dot_general(
                columns[s],
                source[s, :, cut],
                (((0,), (0,)), ((), ())),
                preferred_element_type=jnp.float32,
            )
            for q in range(span // 128):
                mixed[q, pl.ds(s, block, slots), :] = gram[:, q * 128 : (q + 1) * 128] * scale
        for q in range(span // 128):
            lane = slice(n * span + q * 128, n * span + (q + 1) * 128)
            out_ref[:, :, lane] = mixed[q].astype(jnp.bfloat16).reshape(block, slots, 128)


def gram_call(block, gains, own_rows, normalized):
    slots, tokens, width = block.shape
    tile = min(128, own_rows)
    out = pl.pallas_call(
        functools.partial(gram_kernel, own_rows, 1.0 / tokens, normalized),
        grid=(own_rows // tile,),
        out_shape=jax.ShapeDtypeStruct((own_rows, slots, width), jnp.bfloat16),
        in_specs=[
            pl.BlockSpec(block.shape, lambda i: (0, 0, 0), pipeline_mode=pl.Buffered(1)),
            pl.BlockSpec(gains.shape, lambda i: (0, 0, 0), pipeline_mode=pl.Buffered(1)),
        ],
        out_specs=pl.BlockSpec((tile, slots, width), lambda i: (i, 0, 0)),
        scratch_shapes=[
            pltpu.VMEM((slots, tokens, width) if normalized else (slots, 8, 128), jnp.bfloat16),
            pltpu.VMEM((4, tile * slots, 128), jnp.float32),
        ],
        compiler_params=pltpu.CompilerParams(vmem_limit_bytes=min(62 << 20, (32 << 20) + 8 * block.size)),
        name="gram",
    )(block, gains)
    return out.reshape(own_rows, slots, 1, width)


def body(inputs, weights, norm_gains, cotangent):
    micro, rows, width = inputs.shape
    slots = weights.shape[0]
    quarter = weights.shape[3]
    tensors = lax.axis_size("tensor")
    dps = lax.axis_size("dp")
    own_rows = quarter // dps
    tokens = micro * rows * tensors * dps
    h_all, d_all = chain(inputs, weights, norm_gains, cotangent)
    h_all = h_all.reshape(slots, tokens, width)
    d_all = d_all.reshape(slots, tokens, width)
    act = gram_call(h_all, norm_gains, own_rows, True)
    return act, gram_call(d_all, norm_gains, own_rows, False)


def solution(mesh):
    in_specs = (
        P(None, ("tensor", "dp"), None),
        P(None, "pipe", None, "tensor"),
        P(None, "pipe", None),
        P(None, ("tensor", "dp"), None),
    )
    out_specs = (P(("tensor", "dp"), None, "pipe", None), P(("tensor", "dp"), None, "pipe", None))
    return jax.shard_map(body, mesh=mesh, in_specs=in_specs, out_specs=out_specs, check_vma=False)
```

time: 234 us -> 210 us (0.90)
  the two profiles are of different devices: /device:TPU:1 before, /device:TPU:9 now
where the time goes in v1:
time: 210 us
  Pallas kernels  207 us (99%)
  local copies, waits for them, and re-layouts  2.34 us (1%)
    pallas_call x1, Pallas kernels, chain(): pl.pallas_call(functools.partial(chain_kernel, dims), out_shape=(out, out...  185 us
    pallas_call x2, Pallas kernels, gram_call(): pl.pallas_call(functools.partial(gram_kernel, own_rows, 1.0 / tokens, nor...  22.3 us

profile of v1, /device:TPU:9, one launch (start us, length us, event | category | flops | bytes accessed | tf_op | source)
XLA Modules:
  0.0 209.9 jit_solution(10474548904243265330)
XLA Ops:
  0.6 0.0 copy-start.2
  0.6 184.6 %chain.1 = (bf16[2,2,4,32,4096]{4,3,2,1,0:T(8,128)(2,1)}, bf16[2,2,4,32,4096]{4,3,2,1,0:T(8,128)(2,1)}) custom-call(bf16[2,16,4096]{2,1,0:T(8,128)(2,1)} %x_ref.1, bf16[2,1,4096,1024]{3,2,1,0:T(8,128)(2,1)} %w_hbm.1, f32[2,1,4096]{2,1,0:T(1,128)} %g_ref.5, bf16[2,16,4096]{2,1,0:T(8,128)(2,1)} %cot_ref.1), custom_call_target="tpu_custom_call" | custom-call | tf_op jit(solution)/shard_map/chain/pallas_call | solution.py:582
  185.2 0.0 copy-start
  185.2 0.0 copy-done.2
  185.2 0.0 copy-start.1
  185.3 2.3 %copy-done.1 = bf16[2,2,4,32,4096]{4,3,2,1,0:T(8,128)(2,1)S(1)} copy-done((bf16[2,2,4,32,4096]{4,3,2,1,0:T(8,128)(2,1)S(1)}, bf16[2,2,4,32,4096]{4,3,2,1,0:T(8,128)(2,1)}, u32[]{:S(2)}) %copy-start.1) | copy-done | bytes 4194328
  187.6 10.0 %gram.3 = bf16[512,2,4096]{2,1,0:T(2,128)(2,1)} custom-call(bf16[2,256,4096]{2,1,0:T(8,128)(2,1)S(1)} %bitcast.9, f32[2,1,4096]{2,1,0:T(1,128)S(1)} %copy-done.2), custom_call_target="tpu_custom_call" | custom-call | tf_op jit(solution)/shard_map/gram/pallas_call | solution.py:675
  197.6 0.0 copy-done
  197.6 12.3 %gram.2 = bf16[512,2,4096]{2,1,0:T(2,128)(2,1)} custom-call(bf16[2,256,4096]{2,1,0:T(8,128)(2,1)S(1)} %bitcast.8, f32[2,1,4096]{2,1,0:T(1,128)S(1)} %copy-done.2), custom_call_target="tpu_custom_call" | custom-call | tf_op jit(solution)/shard_map/gram/pallas_call | solution.py:675
Async XLA Ops:
  0.6 184.6 %copy-start.2 = (f32[2,1,4096]{2,1,0:T(1,128)S(1)}, f32[2,1,4096]{2,1,0:T(1,128)}, u32[]{:S(2)}) copy-start(f32[2,1,4096]{2,1,0:T(1,128)} %g_ref.5) | copy-start | bytes 98308
  185.2 12.4 %copy-start = (bf16[2,2,4,32,4096]{4,3,2,1,0:T(8,128)(2,1)S(1)}, bf16[2,2,4,32,4096]{4,3,2,1,0:T(8,128)(2,1)}, u32[]{:S(2)}) copy-start(bf16[2,2,4,32,4096]{4,3,2,1,0:T(8,128)(2,1)} %get-tuple-element.4) | copy-start | bytes 12582916
  185.2 2.3 %copy-start.1 = (bf16[2,2,4,32,4096]{4,3,2,1,0:T(8,128)(2,1)S(1)}, bf16[2,2,4,32,4096]{4,3,2,1,0:T(8,128)(2,1)}, u32[]{:S(2)}) copy-start(bf16[2,2,4,32,4096]{4,3,2,1,0:T(8,128)(2,1)} %get-tuple-element.5) | copy-start | bytes 12582916

commit v2 on v1

--- a/solution.py
+++ b/solution.py
@@ -30,16 +30,18 @@
     rms,
     acc,
     nxt,
-    own,
     far_send,
     far_recv,
     near_send,
     near_recv,
-    x_send,
-    x_recv,
-    dnext,
+    a_send,
+    a_recv,
+    b_send,
+    b_recv,
     isend,
     irecv,
+    tsend,
+    trecv,
     w_sem,
     own_sem,
     in_send,
@@ -48,20 +50,22 @@
     f1_recv,
     fx_send,
     fx_recv,
-    b1_send,
-    b1_recv,
+    ab_send,
+    ab_recv,
     s3_send,
     s3_recv,
     s1_send,
     s1_recv,
-    xc_send,
-    xc_recv,
     is_send,
     is_recv,
+    ts_send,
+    ts_recv,
     dp_send,
     dp_recv,
     dg_send,
     dg_recv,
+    dr_send,
+    dr_recv,
     loc_sem,
 ):
     chunks, splits, slots, rows, width, quarter, pipes, tensors, dps, cuts = dims
@@ -96,7 +100,7 @@
 
     barrier = pltpu.get_barrier_semaphore()
     partners = [where(p, peer_of(c, k), d) for k in range(1, tensors)]
-    partners += [where(after, c, d), where(before, c, d)]
+    partners += [where(pp, peer_of(c, k), d) for pp in (after, before) for k in range(tensors)]
     partners += [
         where(p, peer_of(c, k), lax.rem(d + e, dps)) for e in range(1, dps) for k in range(tensors)
     ]
@@ -162,7 +166,7 @@
     def _():
         opening_all(x_ref, hbuf)
 
-    @pl.when(p == pipes - 1)
+    @pl.when(p >= pipes - 2)
     def _():
         opening_all(cot_ref, dcol)
 
@@ -197,38 +201,58 @@
             where(p, peer_of(c, k), lax.rem(d + e, dps)),
         )
 
+    far_shares = [(e, k) for e in range(dps - 1, -1, -1) for k in (2, 0) if e or k]
+
     def d_shares(item, slot, q):
-        return [
-            d_share(item, slot, q, e, k)
-            for e in range(dps - 1, -1, -1)
-            for k in range(tensors - 1, -1, -1)
-            if e or k
-        ]
-
-    def f_along(item, target_item, r):
+        return [d_share(item, slot, q, e, k) for e, k in far_shares + [(0, 1)]]
+
+    def d_relay(item, slot, q, e, k, arriving=False):
+        origin = peer_of(peer_of(c, 1), k) if arriving else peer_of(c, k)
+        ref = d_out.at[slot, lax.rem(d + dps - e, dps), q, :, col_ds(origin)]
+        return remote(
+            ref, ref, dr_send.at[item, e, k], dr_recv.at[item, e, k], where(p, peer_of(c, 1), d)
+        )
+
+    def d_relays(item, slot, q):
+        for e, k in far_shares:
+            d_share(item, slot, q, e, k).wait_recv()
+            d_relay(item, slot, q, e, k).start()
+
+    def f_along(item, target_item, k, r):
         return remote(
             nxt.at[item, :, span(r)],
             hbuf.at[target_item, :, cut_ds(c, r)],
-            f1_send.at[item, r],
-            f1_recv.at[target_item, r],
-            where(after, c, d),
-        )
-
-    def spread(item, part, r):
-        owner = peer_of(c, 2) if part == 2 else c
-        target = peer_of(c, 2) if part == 1 else peer_of(c, 1)
-        ref = hbuf.at[item, :, cut_ds(owner, r)]
-        return remote(
-            ref, ref, fx_send.at[item, part, r], fx_recv.at[item, part, r], where(p, target, d)
-        )
-
-    def b_along(item, target_item, r):
-        return remote(
-            dnext.at[item, :, span(r)],
-            dcol.at[target_item, :, span(r)],
-            b1_send.at[item, r],
-            b1_recv.at[target_item, r],
-            where(before, c, d),
+            f1_send.at[item, k // 2, r],
+            f1_recv.at[target_item, k // 2, r],
+            where(after, peer_of(c, k), d),
+        )
+
+    def f_arrive(item, k, r):
+        ref = hbuf.at[item, :, cut_ds(peer_of(c, k), r)]
+        remote(
+            ref, ref, f1_send.at[item, k // 2, r], f1_recv.at[item, k // 2, r], where(after, c, d)
+        ).wait_recv()
+        spread(item, k, r).start()
+
+    def spread(item, k, r, arriving=False):
+        origin = peer_of(peer_of(c, 1), k) if arriving else peer_of(c, k)
+        ref = hbuf.at[item, :, cut_ds(origin, r)]
+        return remote(
+            ref,
+            ref,
+            fx_send.at[item, k // 2, r],
+            fx_recv.at[item, k // 2, r],
+            where(p, peer_of(c, 1), d),
+        )
+
+    def ab_copy(item, target_item, k, r):
+        src, dst = (b_send, b_recv) if k else (a_send, a_recv)
+        return remote(
+            src.at[item, :, span(r)],
+            dst.at[target_item, :, span(r)],
+            ab_send.at[item, k // 2, r],
+            ab_recv.at[target_item, k // 2, r],
+            where(before, peer_of(c, k), d),
         )
 
     def far_copy(item, r):
@@ -249,145 +273,115 @@
             where(p, peer_of(c, 1), d),
         )
 
-    def x_copy(item, r):
-        return remote(
-            x_send.at[item, :, span(r)],
-            x_recv.at[item, :, span(r)],
-            xc_send.at[item, r],
-            xc_recv.at[item, r],
-            where(p, peer_of(c, 2), d),
-        )
-
-    def inner_copy(item, k):
+    def inner_copy(item, target_item, k):
         return remote(
             isend.at[item],
-            irecv.at[item, k - 1],
-            is_send.at[item, k - 1],
-            is_recv.at[item, k - 1],
+            irecv.at[target_item, k],
+            is_send.at[item, k],
+            is_recv.at[target_item, k],
+            where(before, peer_of(c, k), d),
+        )
+
+    def turn_copy(q, k):
+        return remote(
+            tsend.at[q],
+            trecv.at[q, k - 1],
+            ts_send.at[q, k - 1],
+            ts_recv.at[q, k - 1],
             where(p, peer_of(c, k), d),
         )
 
-    def sums_start(item, first, second):
+    def flat(first, second):
         lanes = [jnp.broadcast_to(v, (group, 128)) for v in (first, second)]
         square = jnp.concatenate([lanes[i % 2] for i in range(128 // group)], axis=0)
-        isend[item] = jnp.transpose(square)[:8]
-        for k in range(tensors - 1, 0, -1):
-            inner_copy(item, k).start()
-
-    def sums_finish(item):
-        for k in range(1, tensors):
-            inner_copy(item, k).wait_recv()
-        sums = isend[item]
-        for k in range(1, tensors):
-            sums += irecv[item, k - 1]
-        upright = jnp.transpose(jnp.concatenate([sums] * 16, axis=0))
-        return upright[:group, :1], upright[group : 2 * group, :1]
+        return jnp.transpose(square)[:8]
+
+    def upright(sums):
+        tall = jnp.transpose(jnp.concatenate([sums] * 16, axis=0))
+        return tall[:group, :1], tall[group : 2 * group, :1]
+
+    def before_item(item):
+        return item + chunks * (1 - (p + pipes - 1) // pipes)
 
     def reduce(item, slot, stored):
+        ahead = stored is None
         columns = dcol[item]
+        target_item = before_item(item)
         inner = jnp.zeros((group, 1), jnp.float32)
+        if not ahead:
+            inverse_rms = rms[stored][:, :1]
         order = [(3, r) for r in range(cuts)] + [(1, 0)] + [(2, r) for r in range(cuts)]
         order += [(1, r) for r in range(1, cuts)] + [(0, r) for r in range(cuts)]
         for k, r in order:
             where_to = cut_ds(peer_of(c, k), r)
+            gain = g_ref[slot, :, where_to]
             term = lax.dot_general(
                 columns,
                 w[slot, where_to, :],
                 (((1,), (1,)), ((), ())),
                 preferred_element_type=jnp.float32,
-            ).astype(jnp.bfloat16)
+            )
             if k == 3:
-                far_send[item, :, span(r)] = term
+                far_send[item, :, span(r)] = term.astype(jnp.bfloat16)
                 far_copy(item, r).start()
+            elif k == 1:
+                near_send[item, :, span(r)] = term.astype(jnp.bfloat16)
+                near_copy(item, r).start()
             elif k == 2:
                 far_copy(item, r).wait_recv()
-                x_send[item, :, span(r)] = (
-                    term.astype(jnp.float32) + far_recv[item, :, span(r)].astype(jnp.float32)
-                ).astype(jnp.bfloat16)
-                x_copy(item, r).start()
-            elif k == 1:
-                near_send[item, :, span(r)] = term
-                near_copy(item, r).start()
+                both = gain * (term + far_recv[item, :, span(r)].astype(jnp.float32))
+                if not ahead:
+                    both = inverse_rms * both
+                b_send[item, :, span(r)] = both.astype(jnp.bfloat16)
+                ab_copy(item, target_item, 2, r).start()
             else:
-                own[item, :, span(r)] = term
-            if stored is not None:
-                scaled = g_ref[slot, :, where_to] * term.astype(jnp.float32)
+                near_copy(item, r).wait_recv()
+                both = gain * (term + near_recv[item, :, span(r)].astype(jnp.float32))
+                if not ahead:
+                    both = dcol[item, :, span(r)].astype(jnp.float32) + inverse_rms * both
+                a_send[item, :, span(r)] = both.astype(jnp.bfloat16)
+                ab_copy(item, target_item, 0, r).start()
+            if not ahead:
                 hidden = hbuf[stored, :, where_to].astype(jnp.float32)
-                inner += jnp.sum(hidden * scaled, axis=-1, keepdims=True)
-        return inner
-
-    def reduce_wait(item, r):
-        near_copy(item, r).wait_recv()
-        x_copy(item, r).wait_recv()
-
-    def back_of(item, r):
-        return (
-            own[item, :, span(r)].astype(jnp.float32)
-            + near_recv[item, :, span(r)].astype(jnp.float32)
-            + x_recv[item, :, span(r)].astype(jnp.float32)
-        )
-
-    def finalize(item, slot, stored, inner_all, inverse_rms, waiting):
-        factor = inverse_rms * inverse_rms * inverse_rms * (inner_all * (1.0 / width))
-        target_item = item + chunks * (1 - (p + pipes - 1) // pipes)
-        for r in range(cuts):
-            if waiting:
-                reduce_wait(item, r)
-            dnext[item, :, span(r)] = (
-                dcol[item, :, span(r)].astype(jnp.float32)
-                + inverse_rms * (g_ref[slot, :, cut_ds(c, r)] * back_of(item, r))
-                - factor * hbuf[stored, :, cut_ds(c, r)].astype(jnp.float32)
-            ).astype(jnp.bfloat16)
-            b_along(item, target_item, r).start()
+                inner += jnp.sum(hidden * (gain * term), axis=-1, keepdims=True)
+        if not ahead:
+            factor = inverse_rms * inverse_rms * inverse_rms * (inner * (1.0 / width))
+            isend[item] = flat(factor, factor)
+            for k in (2, 3, 0, 1):
+                inner_copy(item, target_item, k).start()
 
     def turn_ahead(q, carry):
         opening_wait(cot_ref, dcol, q)
-        d_own(q, slots - 1, q).start()
         reduce(q, slots - 1, None)
-        for r in range(cuts):
-            reduce_wait(q, r)
         return carry
 
-    def turn_after(q, carry):
-        item = (slots - 1) * chunks + q
-        for r in range(cuts):
-            spread(item, 1, r).wait_recv()
-            spread(item, 2, r).start()
-        for r in range(cuts):
-            spread(item, 0, r).wait_recv()
-            spread(item, 2, r).wait_recv()
-        h_shares(item, slots - 1, q)
-        for share in d_shares(q, slots - 1, q):
-            share.start()
-        return carry
-
-    def f_step(item, carry):
+    def step(t, carry):
+        f_on = t < items
+        item = jnp.minimum(t, items - 1)
         slot = item // chunks
         q = lax.rem(item, chunks)
         layer = slot * pipes + p
         target_item = item + chunks * ((p + 1) // pipes)
 
-        @pl.when((layer == layers - 1) & (q == 0))
+        @pl.when(f_on & (layer == layers - 1) & (q == 0))
         def _():
             w_copy(slots - 1).wait()
             lax.fori_loop(0, chunks, turn_ahead, 0)
 
-        @pl.when((layer < layers - 1) & (q == 0))
+        @pl.when(f_on & (layer < layers - 1) & (q == 0))
         def _():
             w_copy(slot).wait()
 
-        @pl.when(layer == 0)
+        @pl.when(f_on & (layer == 0))
         def _():
             opening_wait(x_ref, hbuf, item)
 
-        @pl.when(layer > 0)
-        def _():
-            for r in range(cuts):
-                f_along(item, item, r).wait_recv()
-                spread(item, 1, r).start()
-                spread(item, 0, r).start()
-
-        @pl.when(layer < layers - 1)
+        @pl.when(f_on & (layer > 0))
+        def _():
+            for r in range(cuts):
+                f_arrive(item, 0, r)
+
+        @pl.when(f_on & (layer < layers - 1))
         def _():
             def scaled_of(cc, r):
                 part = hbuf[item, :, cut_ds(cc, r)].astype(jnp.float32)
@@ -408,29 +402,25 @@
             total = piece(c, 0, True)
             for r in range(1, cuts):
                 total += piece(c, r)
-
-            @pl.when(layer > 0)
-            def _():
-                for r in range(cuts):
-                    spread(item, 0, r).wait_recv()
-
-            for r in range(cuts):
-                total += piece(peer_of(c, 1), r)
-
             for r in range(cuts):
 
                 @pl.when(layer > 0)
                 def _(r=r):
-                    spread(item, 1, r).wait_recv()
-                    spread(item, 2, r).start()
+                    f_arrive(item, 2, r)
 
                 total += piece(peer_of(c, 2), r)
-
             for r in range(cuts):
 
                 @pl.when(layer > 0)
                 def _(r=r):
-                    spread(item, 2, r).wait_recv()
+                    spread(item, 0, r, True).wait_recv()
+
+                total += piece(peer_of(c, 1), r)
+            for r in range(cuts):
+
+                @pl.when(layer > 0)
+                def _(r=r):
+                    spread(item, 2, r, True).wait_recv()
 
                 if r < cuts - 1:
                     total += piece(peer_of(c, 3), r)
@@ -446,68 +436,114 @@
                 nxt[item, :, span(n)] = (
                     hbuf[item, :, cut_ds(c, n)].astype(jnp.float32) + product
                 ).astype(jnp.bfloat16)
-                f_along(item, target_item, n).start()
+                f_along(item, target_item, 2, n).start()
+                f_along(item, target_item, 0, n).start()
             rms[item] = jnp.broadcast_to(inverse_rms, (group, 128))
-            h_shares(item, slot, q)
-
-        @pl.when(layer == layers - 1)
-        def _():
+
+        @pl.when(f_on & (layer == layers - 2))
+        def _():
+            opening_wait(cot_ref, dcol, q)
             inner = jnp.zeros((group, 1), jnp.float32)
             square = jnp.zeros((group, 1), jnp.float32)
             for r in range(cuts):
-                hidden = hbuf[item, :, cut_ds(c, r)].astype(jnp.float32)
-                scaled = g_ref[slot, :, cut_ds(c, r)] * back_of(q, r)
-                inner += jnp.sum(hidden * scaled, axis=-1, keepdims=True)
+                for k in (0, 2):
+                    ab_copy(q, q, k, r).wait_recv()
+                hidden = nxt[item, :, span(r)].astype(jnp.float32)
+                back = a_recv[q, :, span(r)].astype(jnp.float32)
+                back += b_recv[q, :, span(r)].astype(jnp.float32)
+                inner += jnp.sum(hidden * back, axis=-1, keepdims=True)
                 square += jnp.sum(hidden * hidden, axis=-1, keepdims=True)
-            sums_start(q, inner, square)
-            inner_all, square_all = sums_finish(q)
-            inverse_rms = lax.rsqrt(square_all * (1.0 / width) + EPSILON)
-            finalize(q, slot, item, inner_all, inverse_rms, False)
-
-        @pl.when((layer == layers - 1) & (q == chunks - 1))
-        def _():
-            lax.fori_loop(0, chunks, turn_after, 0)
-
+            tsend[q] = flat(inner, square)
+            for k in (2, 3, 1):
+                turn_copy(q, k).start()
+
+        @pl.when(f_on & (layer == layers - 1))
+        def _():
+            for r in range(cuts):
+                f_arrive(item, 2, r)
+            for r in range(cuts):
+                spread(item, 0, r, True).wait_recv()
+                spread(item, 2, r, True).wait_recv()
+
+        @pl.when(f_on)
+        def _():
+            h_shares(item, slot, q)
+
+        b_step(t)
         return carry
 
-    lax.fori_loop(0, items, f_step, 0)
-
-    def b_step(item, carry):
+    def b_step(t):
+        early = jnp.where(p == pipes - 2, chunks - 1, 0)
+        b_time = t - (items - early)
+        b_on = (b_time >= 0) & (b_time < items)
+        item = jnp.clip(b_time, 0, items - 1)
         slot = slots - 1 - item // chunks
         q = lax.rem(item, chunks)
         layer = slot * pipes + p
         stored = slot * chunks + q
 
-        @pl.when(layer < layers - 1)
-        def _():
-            for r in range(cuts):
-                b_along(item, item, r).wait_recv()
-
-        @pl.when(layer == 0)
+        @pl.when(b_on & (q == 0) & (slot < slots - 1))
+        def _():
+            for back in range(chunks):
+                d_relays(item - chunks + back, slot + 1, back)
+
+        @pl.when(b_on & (layer == layers - 2))
+        def _():
+            for k in range(1, tensors):
+                turn_copy(q, k).wait_recv()
+            sums = tsend[q]
+            for k in range(1, tensors):
+                sums += trecv[q, k - 1]
+            inner, square = upright(sums)
+            inverse_rms = lax.rsqrt(square * (1.0 / width) + EPSILON)
+            factor = inverse_rms * inverse_rms * inverse_rms * (inner * (1.0 / width))
+            for r in range(cuts):
+                back = a_recv[item, :, span(r)].astype(jnp.float32)
+                back += b_recv[item, :, span(r)].astype(jnp.float32)
+                dcol[item, :, span(r)] = (
+                    dcol[item, :, span(r)].astype(jnp.float32)
+                    + inverse_rms * back
+                    - factor * nxt[stored, :, span(r)].astype(jnp.float32)
+                ).astype(jnp.bfloat16)
+
+        @pl.when(b_on & (layer < layers - 2))
+        def _():
+            for k in range(tensors):
+                inner_copy(item, item, k).wait_recv()
+            sums = irecv[item, 0]
+            for k in range(1, tensors):
+                sums += irecv[item, k]
+            factor, _ = upright(sums)
+            for r in range(cuts):
+                for k in (2, 0):
+                    ab_copy(item, item, k, r).wait_recv()
+                dcol[item, :, span(r)] = (
+                    a_recv[item, :, span(r)].astype(jnp.float32)
+                    + b_recv[item, :, span(r)].astype(jnp.float32)
+                    - factor * nxt[stored, :, span(r)].astype(jnp.float32)
+                ).astype(jnp.bfloat16)
+
+        @pl.when(b_on & (layer > 0) & (layer < layers - 1))
+        def _():
+            reduce(item, slot, stored)
+
+        @pl.when(b_on & (layer == 0))
         def _():
             for share in d_shares(item, slot, q):
                 share.start()
-
-        @pl.when(layer < layers - 1)
-        def _():
             d_own(item, slot, q).start()
 
-        @pl.when((layer > 0) & (layer < layers - 1))
-        def _():
-            inner = reduce(item, slot, stored)
-            sums_start(item, inner, inner)
-            inner_all, _ = sums_finish(item)
-            finalize(item, slot, stored, inner_all, rms[stored][:, :1], True)
-
-        @pl.when((layer > 0) & (layer < layers - 1) & (q == chunks - 1))
+        @pl.when(b_on & (layer > 0) & (q == chunks - 1))
         def _():
             for back in range(chunks):
                 for share in d_shares(item - (chunks - 1) + back, slot, back):
                     share.start()
-
-        return carry
-
-    lax.fori_loop(0, items, b_step, 0)
+                d_own(item - (chunks - 1) + back, slot, back).start()
+
+    lax.fori_loop(0, 2 * items, step, 0)
+
+    for back in range(chunks):
+        d_relays((slots - 1) * chunks + back, 0, back)
 
     @pl.when(p == 0)
     def _():
@@ -515,7 +551,7 @@
             for k in range(1, tensors):
                 opening(x_ref, hbuf, q, k).wait_send()
 
-    @pl.when(p == pipes - 1)
+    @pl.when(p >= pipes - 2)
     def _():
         for q in range(chunks):
             for k in range(1, tensors):
@@ -530,31 +566,43 @@
 
         @pl.when(f_layer > 0)
         def _():
-            for part in range(3):
+            for k in (0, 2):
                 for r in range(cuts):
-                    spread(item, part, r).wait_send()
+                    spread(item, k, r).wait_send()
 
         @pl.when(f_layer < layers - 1)
         def _():
-            for r in range(cuts):
-                f_along(item, item, r).wait_send()
+            for k in (0, 2):
+                for r in range(cuts):
+                    f_along(item, item, k, r).wait_send()
 
         @pl.when(b_layer > 0)
         def _():
             for r in range(cuts):
-                b_along(item, item, r).wait_send()
+                for k in (0, 2):
+                    ab_copy(item, item, k, r).wait_send()
                 far_copy(item, r).wait_send()
                 near_copy(item, r).wait_send()
-                x_copy(item, r).wait_send()
+
+        @pl.when((b_layer > 0) & (b_layer < layers - 1))
+        def _():
+            for k in range(tensors):
+                inner_copy(item, item, k).wait_send()
+
+        @pl.when(b_layer == layers - 2)
+        def _():
             for k in range(1, tensors):
-                inner_copy(item, k).wait_send()
+                turn_copy(q, k).wait_send()
 
         to_own(item, f_slot, q).wait()
         d_own(item, b_slot, q).wait()
         for k in range(1, dps):
             to_dp(item, f_slot, q, k).wait()
-        for share in d_shares(item, b_slot, q):
-            share.wait()
+        for e, k in far_shares:
+            d_share(item, b_slot, q, e, k).wait_send()
+            d_relay(item, b_slot, q, e, k).wait_send()
+            d_relay(item, b_slot, q, e, k, True).wait_recv()
+        d_share(item, b_slot, q, 0, 1).wait()
         return carry
 
     lax.fori_loop(0, items, ending, 0)
@@ -600,27 +648,31 @@
             piece,
             piece,
             pltpu.VMEM((items, 8, 128), jnp.float32),
-            pltpu.VMEM((items, tensors - 1, 8, 128), jnp.float32),
+            pltpu.VMEM((items, tensors, 8, 128), jnp.float32),
+            pltpu.VMEM((chunks, 8, 128), jnp.float32),
+            pltpu.VMEM((chunks, tensors - 1, 8, 128), jnp.float32),
             dma((slots,)),
             dma((chunks,)),
             dma((chunks, tensors - 1)),
             dma((chunks, tensors - 1)),
-            dma((items, cuts)),
-            dma((items, cuts)),
-            dma((items, 3, cuts)),
-            dma((items, 3, cuts)),
+            dma((items, 2, cuts)),
+            dma((items, 2, cuts)),
+            dma((items, 2, cuts)),
+            dma((items, 2, cuts)),
+            dma((items, 2, cuts)),
+            dma((items, 2, cuts)),
             dma((items, cuts)),
             dma((items, cuts)),
             dma((items, cuts)),
             dma((items, cuts)),
-            dma((items, cuts)),
-            dma((items, cuts)),
-            dma((items, cuts)),
-            dma((items, cuts)),
-            dma((items, tensors - 1)),
-            dma((items, tensors - 1)),
+            dma((items, tensors)),
+            dma((items, tensors)),
+            dma((chunks, tensors - 1)),
+            dma((chunks, tensors - 1)),
             dma((items, dps - 1)),
             dma((items, dps - 1)),
+            dma((items, dps, tensors)),
+            dma((items, dps, tensors)),
             dma((items, dps, tensors)),
             dma((items, dps, tensors)),
             dma((2, items)),

time: 210 us -> 172 us (0.82)
  the two profiles are of different devices: /device:TPU:9 before, /device:TPU:1 now
where the time goes in v2:
time: 172 us; the launch traced here: 169 us
  Pallas kernels  166 us (97%)
  local copies, waits for them, and re-layouts  2.34 us (1%)
    pallas_call x1, Pallas kernels, chain(): pl.pallas_call(functools.partial(chain_kernel, dims), out_shape=(out, out...  144 us
    pallas_call x2, Pallas kernels, gram_call(): pl.pallas_call(functools.partial(gram_kernel, own_rows, 1.0 / tokens, nor...  22.3 us

profile of v2, /device:TPU:1, one launch (start us, length us, event | category | flops | bytes accessed | tf_op | source)
XLA Modules:
  0.0 169.0 jit_solution(4175545057543491540)
XLA Ops:
  0.6 0.0 copy-start.2
  0.6 143.7 %chain.1 = (bf16[2,2,4,32,4096]{4,3,2,1,0:T(8,128)(2,1)}, bf16[2,2,4,32,4096]{4,3,2,1,0:T(8,128)(2,1)}) custom-call(bf16[2,16,4096]{2,1,0:T(8,128)(2,1)} %x_ref.1, bf16[2,1,4096,1024]{3,2,1,0:T(8,128)(2,1)} %w_hbm.1, f32[2,1,4096]{2,1,0:T(1,128)} %g_ref.5, bf16[2,16,4096]{2,1,0:T(8,128)(2,1)} %cot_ref.1), custom_call_target="tpu_custom_call" | custom-call | tf_op jit(solution)/shard_map/chain/pallas_call | solution.py:630
  144.4 0.0 copy-start
  144.4 0.0 copy-done.2
  144.4 0.0 copy-start.1
  144.4 2.3 %copy-done.1 = bf16[2,2,4,32,4096]{4,3,2,1,0:T(8,128)(2,1)S(1)} copy-done((bf16[2,2,4,32,4096]{4,3,2,1,0:T(8,128)(2,1)S(1)}, bf16[2,2,4,32,4096]{4,3,2,1,0:T(8,128)(2,1)}, u32[]{:S(2)}) %copy-start.1) | copy-done | bytes 4194328
  146.7 10.0 %gram.3 = bf16[512,2,4096]{2,1,0:T(2,128)(2,1)} custom-call(bf16[2,256,4096]{2,1,0:T(8,128)(2,1)S(1)} %bitcast.9, f32[2,1,4096]{2,1,0:T(1,128)S(1)} %copy-done.2), custom_call_target="tpu_custom_call" | custom-call | tf_op jit(solution)/shard_map/gram/pallas_call | solution.py:727
  156.8 0.0 copy-done
  156.8 12.3 %gram.2 = bf16[512,2,4096]{2,1,0:T(2,128)(2,1)} custom-call(bf16[2,256,4096]{2,1,0:T(8,128)(2,1)S(1)} %bitcast.8, f32[2,1,4096]{2,1,0:T(1,128)S(1)} %copy-done.2), custom_call_target="tpu_custom_call" | custom-call | tf_op jit(solution)/shard_map/gram/pallas_call | solution.py:727
Async XLA Ops:
  0.6 143.8 %copy-start.2 = (f32[2,1,4096]{2,1,0:T(1,128)S(1)}, f32[2,1,4096]{2,1,0:T(1,128)}, u32[]{:S(2)}) copy-start(f32[2,1,4096]{2,1,0:T(1,128)} %g_ref.5) | copy-start | bytes 98308
  144.4 12.4 %copy-start = (bf16[2,2,4,32,4096]{4,3,2,1,0:T(8,128)(2,1)S(1)}, bf16[2,2,4,32,4096]{4,3,2,1,0:T(8,128)(2,1)}, u32[]{:S(2)}) copy-start(bf16[2,2,4,32,4096]{4,3,2,1,0:T(8,128)(2,1)} %get-tuple-element.4) | copy-start | bytes 12582916
  144.4 2.3 %copy-start.1 = (bf16[2,2,4,32,4096]{4,3,2,1,0:T(8,128)(2,1)S(1)}, bf16[2,2,4,32,4096]{4,3,2,1,0:T(8,128)(2,1)}, u32[]{:S(2)}) copy-start(bf16[2,2,4,32,4096]{4,3,2,1,0:T(8,128)(2,1)} %get-tuple-element.5) | copy-start | bytes 12582916

commit v3 on v2

--- a/solution.py
+++ b/solution.py
@@ -9,7 +9,7 @@
 
 EPSILON = 1e-05
 SPLITS = 2
-CUTS = 2
+CUTS = 1
 
 
 def peer_of(c, k):
@@ -25,8 +25,10 @@
     h_out,
     d_out,
     w,
+    w_t,
     hbuf,
     dcol,
+    d_all,
     rms,
     acc,
     nxt,
@@ -189,13 +191,13 @@
 
     def d_own(item, slot, q):
         return pltpu.make_async_copy(
-            dcol.at[item], d_out.at[slot, d, q, :, col_ds(c)], loc_sem.at[1, item]
+            dcol.at[item], d_all.at[slot, d, q, :, col_ds(c)], loc_sem.at[1, item]
         )
 
     def d_share(item, slot, q, e, k):
         return remote(
             dcol.at[item],
-            d_out.at[slot, d, q, :, col_ds(c)],
+            d_all.at[slot, d, q, :, col_ds(c)],
             dg_send.at[item, e, k],
             dg_recv.at[item, e, k],
             where(p, peer_of(c, k), lax.rem(d + e, dps)),
@@ -206,9 +208,15 @@
     def d_shares(item, slot, q):
         return [d_share(item, slot, q, e, k) for e, k in far_shares + [(0, 1)]]
 
+    def d_shares_all(first, slot):
+        for q in range(chunks):
+            for share in d_shares(first + q, slot, q):
+                share.start()
+            d_own(first + q, slot, q).start()
+
     def d_relay(item, slot, q, e, k, arriving=False):
         origin = peer_of(peer_of(c, 1), k) if arriving else peer_of(c, k)
-        ref = d_out.at[slot, lax.rem(d + dps - e, dps), q, :, col_ds(origin)]
+        ref = d_all.at[slot, lax.rem(d + dps - e, dps), q, :, col_ds(origin)]
         return remote(
             ref, ref, dr_send.at[item, e, k], dr_recv.at[item, e, k], where(p, peer_of(c, 1), d)
         )
@@ -217,6 +225,18 @@
         for e, k in far_shares:
             d_share(item, slot, q, e, k).wait_recv()
             d_relay(item, slot, q, e, k).start()
+
+    def d_flush(item, slot, q):
+        return pltpu.make_async_copy(
+            d_all.at[slot, :, q], d_out.at[slot, :, q], loc_sem.at[2, item]
+        )
+
+    def d_gather(item, slot, q):
+        d_own(item, slot, q).wait()
+        for e, k in far_shares:
+            d_relay(item, slot, q, e, k, True).wait_recv()
+        d_share(item, slot, q, 0, 1).wait_recv()
+        d_flush(item, slot, q).start()
 
     def f_along(item, target_item, k, r):
         return remote(
@@ -315,12 +335,7 @@
         for k, r in order:
             where_to = cut_ds(peer_of(c, k), r)
             gain = g_ref[slot, :, where_to]
-            term = lax.dot_general(
-                columns,
-                w[slot, where_to, :],
-                (((1,), (1,)), ((), ())),
-                preferred_element_type=jnp.float32,
-            )
+            term = jnp.dot(columns, w_t[slot, :, where_to], preferred_element_type=jnp.float32)
             if k == 3:
                 far_send[item, :, span(r)] = term.astype(jnp.bfloat16)
                 far_copy(item, r).start()
@@ -350,6 +365,16 @@
             for k in (2, 3, 0, 1):
                 inner_copy(item, target_item, k).start()
 
+    def turn_over(s):
+        side = 256
+
+        def block(i, carry):
+            part = pl.ds(pl.multiple_of(i * side, side), side)
+            w_t[s, :, part] = jnp.transpose(w[s, part, :])
+            return carry
+
+        lax.fori_loop(0, width // side, block, 0)
+
     def turn_ahead(q, carry):
         opening_wait(cot_ref, dcol, q)
         reduce(q, slots - 1, None)
@@ -363,14 +388,21 @@
         layer = slot * pipes + p
         target_item = item + chunks * ((p + 1) // pipes)
 
-        @pl.when(f_on & (layer == layers - 1) & (q == 0))
-        def _():
-            w_copy(slots - 1).wait()
-            lax.fori_loop(0, chunks, turn_ahead, 0)
-
-        @pl.when(f_on & (layer < layers - 1) & (q == 0))
+        @pl.when(f_on & (q == 0))
         def _():
             w_copy(slot).wait()
+
+        @pl.when(f_on & (q == 0) & (slot == slots - 1))
+        def _():
+            turn_over(slots - 1)
+
+            @pl.when(layer == layers - 1)
+            def _():
+                lax.fori_loop(0, chunks, turn_ahead, 0)
+                d_shares_all(0, slots - 1)
+
+            for s in range(slots - 1):
+                turn_over(s)
 
         @pl.when(f_on & (layer == 0))
         def _():
@@ -486,6 +518,8 @@
         def _():
             for back in range(chunks):
                 d_relays(item - chunks + back, slot + 1, back)
+            for back in range(chunks):
+                d_gather(item - chunks + back, slot + 1, back)
 
         @pl.when(b_on & (layer == layers - 2))
         def _():
@@ -527,23 +561,34 @@
         def _():
             reduce(item, slot, stored)
 
-        @pl.when(b_on & (layer == 0))
+        @pl.when(b_on & (slot == 0))
         def _():
             for share in d_shares(item, slot, q):
                 share.start()
             d_own(item, slot, q).start()
 
-        @pl.when(b_on & (layer > 0) & (q == chunks - 1))
-        def _():
-            for back in range(chunks):
-                for share in d_shares(item - (chunks - 1) + back, slot, back):
-                    share.start()
-                d_own(item - (chunks - 1) + back, slot, back).start()
+        @pl.when(b_on & (layer == 0) & (q > 0))
+        def _():
+            d_relays(item - 1, slot, q - 1)
+
+        @pl.when(b_on & (slot > 0) & (layer < layers - 1) & (q == chunks - 1))
+        def _():
+            d_shares_all(item - (chunks - 1), slot)
 
     lax.fori_loop(0, 2 * items, step, 0)
 
-    for back in range(chunks):
-        d_relays((slots - 1) * chunks + back, 0, back)
+    for q in range(chunks):
+        item = (slots - 1) * chunks + q
+        if q == chunks - 1:
+            d_relays(item, 0, q)
+        else:
+
+            @pl.when(p > 0)
+            def _(item=item, q=q):
+                d_relays(item, 0, q)
+
+    for q in range(chunks):
+        d_gather((slots - 1) * chunks + q, 0, q)
 
     @pl.when(p == 0)
     def _():
@@ -595,14 +640,13 @@
                 turn_copy(q, k).wait_send()
 
         to_own(item, f_slot, q).wait()
-        d_own(item, b_slot, q).wait()
+        d_flush(item, b_slot, q).wait()
         for k in range(1, dps):
             to_dp(item, f_slot, q, k).wait()
         for e, k in far_shares:
             d_share(item, b_slot, q, e, k).wait_send()
             d_relay(item, b_slot, q, e, k).wait_send()
-            d_relay(item, b_slot, q, e, k, True).wait_recv()
-        d_share(item, b_slot, q, 0, 1).wait()
+        d_share(item, b_slot, q, 0, 1).wait_send()
         return carry
 
     lax.fori_loop(0, items, ending, 0)
@@ -634,8 +678,10 @@
         out_specs=(hbm, hbm),
         scratch_shapes=[
             pltpu.VMEM((slots, width, quarter), jnp.bfloat16),
+            pltpu.VMEM((slots, quarter, width), jnp.bfloat16),
             pltpu.VMEM((items, group, width), jnp.bfloat16),
             piece,
+            pltpu.VMEM((slots, dps, chunks, group, width), jnp.bfloat16),
             pltpu.VMEM((items, group, 128), jnp.float32),
             pltpu.VMEM((group, quarter), jnp.float32),
             piece,
@@ -675,10 +721,10 @@
             dma((items, dps, tensors)),
             dma((items, dps, tensors)),
             dma((items, dps, tensors)),
-            dma((2, items)),
+            dma((3, items)),
         ],
         compiler_params=pltpu.CompilerParams(
-            collective_id=0, has_side_effects=True, vmem_limit_bytes=56 * 1024 * 1024
+            collective_id=0, has_side_effects=True, vmem_limit_bytes=62 * 1024 * 1024
         ),
         name="chain",
     )(inputs, weights, norm_gains, cotangent)

time: 172 us -> 157 us (0.913); the launches traced: 169 us -> 157 us
  Pallas kernels: 166 us -> 154 us
    pallas_call x1, Pallas kernels: 144 us -> 131 us  [chain(): pl.pallas_call(functools.partial(chain_kernel, dims), out_shape=(out, out...]
where the time goes in v3:
time: 157 us
  Pallas kernels  154 us (98%)
  local copies, waits for them, and re-layouts  2.34 us (1%)
    pallas_call x1, Pallas kernels, chain(): pl.pallas_call(functools.partial(chain_kernel, dims), out_shape=(out, out...  131 us
    pallas_call x2, Pallas kernels, gram_call(): pl.pallas_call(functools.partial(gram_kernel, own_rows, 1.0 / tokens, nor...  22.3 us

profile of v3, /device:TPU:1, one launch (start us, length us, event | category | flops | bytes accessed | tf_op | source)
XLA Modules:
  0.0 156.6 jit_solution(4031076299042022435)
XLA Ops:
  0.6 0.0 copy-start.2
  0.6 131.3 %chain.1 = (bf16[2,2,4,32,4096]{4,3,2,1,0:T(8,128)(2,1)}, bf16[2,2,4,32,4096]{4,3,2,1,0:T(8,128)(2,1)}) custom-call(bf16[2,16,4096]{2,1,0:T(8,128)(2,1)} %x_ref.1, bf16[2,1,4096,1024]{3,2,1,0:T(8,128)(2,1)} %w_hbm.1, f32[2,1,4096]{2,1,0:T(1,128)} %g_ref.5, bf16[2,16,4096]{2,1,0:T(8,128)(2,1)} %cot_ref.1), custom_call_target="tpu_custom_call" | custom-call | tf_op jit(solution)/shard_map/chain/pallas_call | solution.py:674
  131.9 0.0 copy-start
  131.9 0.0 copy-done.2
  131.9 0.0 copy-start.1
  132.0 2.3 %copy-done.1 = bf16[2,2,4,32,4096]{4,3,2,1,0:T(8,128)(2,1)S(1)} copy-done((bf16[2,2,4,32,4096]{4,3,2,1,0:T(8,128)(2,1)S(1)}, bf16[2,2,4,32,4096]{4,3,2,1,0:T(8,128)(2,1)}, u32[]{:S(2)}) %copy-start.1) | copy-done | bytes 4194328
  134.3 10.0 %gram.3 = bf16[512,2,4096]{2,1,0:T(2,128)(2,1)} custom-call(bf16[2,256,4096]{2,1,0:T(8,128)(2,1)S(1)} %bitcast.9, f32[2,1,4096]{2,1,0:T(1,128)S(1)} %copy-done.2), custom_call_target="tpu_custom_call" | custom-call | tf_op jit(solution)/shard_map/gram/pallas_call | solution.py:773
  144.3 0.0 copy-done
  144.3 12.3 %gram.2 = bf16[512,2,4096]{2,1,0:T(2,128)(2,1)} custom-call(bf16[2,256,4096]{2,1,0:T(8,128)(2,1)S(1)} %bitcast.8, f32[2,1,4096]{2,1,0:T(1,128)S(1)} %copy-done.2), custom_call_target="tpu_custom_call" | custom-call | tf_op jit(solution)/shard_map/gram/pallas_call | solution.py:773
Async XLA Ops:
  0.6 131.3 %copy-start.2 = (f32[2,1,4096]{2,1,0:T(1,128)S(1)}, f32[2,1,4096]{2,1,0:T(1,128)}, u32[]{:S(2)}) copy-start(f32[2,1,4096]{2,1,0:T(1,128)} %g_ref.5) | copy-start | bytes 98308
  131.9 12.4 %copy-start = (bf16[2,2,4,32,4096]{4,3,2,1,0:T(8,128)(2,1)S(1)}, bf16[2,2,4,32,4096]{4,3,2,1,0:T(8,128)(2,1)}, u32[]{:S(2)}) copy-start(bf16[2,2,4,32,4096]{4,3,2,1,0:T(8,128)(2,1)} %get-tuple-element.4) | copy-start | bytes 12582916
  131.9 2.3 %copy-start.1 = (bf16[2,2,4,32,4096]{4,3,2,1,0:T(8,128)(2,1)S(1)}, bf16[2,2,4,32,4096]{4,3,2,1,0:T(8,128)(2,1)}, u32[]{:S(2)}) copy-start(bf16[2,2,4,32,4096]{4,3,2,1,0:T(8,128)(2,1)} %get-tuple-element.5) | copy-start | bytes 12582916

commit v4 on v3

--- a/solution.py
+++ b/solution.py
@@ -10,6 +10,7 @@
 EPSILON = 1e-05
 SPLITS = 2
 CUTS = 1
+SPAN = 1024
 
 
 def peer_of(c, k):
@@ -27,6 +28,7 @@
     w,
     w_t,
     hbuf,
+    normed,
     dcol,
     d_all,
     rms,
@@ -174,7 +176,7 @@
 
     def to_dp(item, slot, q, k):
         return remote(
-            hbuf.at[item],
+            normed.at[item],
             h_out.at[slot, d, q],
             dp_send.at[item, k - 1],
             dp_recv.at[item, k - 1],
@@ -182,7 +184,7 @@
         )
 
     def to_own(item, slot, q):
-        return pltpu.make_async_copy(hbuf.at[item], h_out.at[slot, d, q], loc_sem.at[0, item])
+        return pltpu.make_async_copy(normed.at[item], h_out.at[slot, d, q], loc_sem.at[0, item])
 
     def h_shares(item, slot, q):
         to_own(item, slot, q).start()
@@ -497,11 +499,23 @@
                 spread(item, 0, r, True).wait_recv()
                 spread(item, 2, r, True).wait_recv()
 
-        @pl.when(f_on)
-        def _():
-            h_shares(item, slot, q)
-
         b_step(t)
+
+        for s in range(slots):
+            late = jnp.where(p == pipes - 2, 1, 0) if s == slots - 1 else 0
+
+            @pl.when(t == (s + 1) * chunks - 1 + late)
+            def _(s=s):
+                lax.fori_loop(s * chunks, (s + 1) * chunks, normalize, 0)
+
+        return carry
+
+    def normalize(item, carry):
+        slot = item // chunks
+        wide = hbuf[item].astype(jnp.float32)
+        mean = jnp.mean(wide * wide, axis=-1, keepdims=True)
+        normed[item] = (wide * lax.rsqrt(mean + EPSILON) * g_ref[slot]).astype(jnp.bfloat16)
+        h_shares(item, slot, lax.rem(item, chunks))
         return carry
 
     def b_step(t):
@@ -679,6 +693,7 @@
         scratch_shapes=[
             pltpu.VMEM((slots, width, quarter), jnp.bfloat16),
             pltpu.VMEM((slots, quarter, width), jnp.bfloat16),
+            pltpu.VMEM((items, group, width), jnp.bfloat16),
             pltpu.VMEM((items, group, width), jnp.bfloat16),
             piece,
             pltpu.VMEM((slots, dps, chunks, group, width), jnp.bfloat16),
@@ -730,63 +745,71 @@
     )(inputs, weights, norm_gains, cotangent)
 
 
-def gram_kernel(base_rows, scale, normalized, x_ref, g_ref, out_ref, full, mixed):
-    slots, tokens, width = x_ref.shape
-    block = out_ref.shape[0]
-    step = pl.program_id(0)
-
-    if normalized:
-
-        @pl.when(step == 0)
-        def _():
+def gram_kernel(base_rows, scale, h_hbm, d_hbm, h_ref, d_ref, act_ref, grad_ref, own, lhs, sem):
+    slots, tokens, span = h_ref.shape
+    lanes = 128
+    mixed = lanes * slots
+
+    @pl.when(pl.program_id(0) == 0)
+    def _():
+        place = lax.axis_index("tensor") * lax.axis_size("dp") + lax.axis_index("dp")
+        columns = pl.ds(pl.multiple_of(place * base_rows, base_rows), base_rows)
+        copies = [
+            pltpu.make_async_copy(source.at[:, :, columns], own.at[i], sem.at[i])
+            for i, source in enumerate((h_hbm, d_hbm))
+        ]
+        for copy in copies:
+            copy.start()
+        row = lax.broadcasted_iota(jnp.int32, (mixed, lanes), 0)
+        column = lax.broadcasted_iota(jnp.int32, (mixed, lanes), 1)
+        for i in range(2):
+            copies[i].wait()
             for s in range(slots):
-                for t in range(0, tokens, 32):
-                    wide = x_ref[s, t : t + 32].astype(jnp.float32)
-                    mean = jnp.mean(wide * wide, axis=-1, keepdims=True)
-                    inverse_rms = lax.rsqrt(mean + EPSILON)
-                    full[s, t : t + 32] = (wide * inverse_rms * g_ref[s]).astype(jnp.bfloat16)
-
-    source = full if normalized else x_ref
-    own = (lax.axis_index("tensor") * lax.axis_size("dp") + lax.axis_index("dp")) * base_rows
-    start = pl.multiple_of(own + step * block, block)
-    columns = [source[s, :, pl.ds(start, block)] for s in range(slots)]
-    span = 512
-    for n in range(width // span):
-        cut = slice(n * span, (n + 1) * span)
-        for s in range(slots):
-            gram = lax.dot_general(
-                columns[s],
-                source[s, :, cut],
-                (((0,), (0,)), ((), ())),
-                preferred_element_type=jnp.float32,
+                pick = jnp.where(row == column * slots + s, 1.0, 0.0).astype(jnp.bfloat16)
+                for b in range(base_rows // lanes):
+                    spread = lax.dot_general(
+                        pick,
+                        own[i, s, :, b * lanes : (b + 1) * lanes],
+                        (((1,), (1,)), ((), ())),
+                        preferred_element_type=jnp.float32,
+                    )
+                    lhs[i, b * mixed : (b + 1) * mixed, s * tokens : (s + 1) * tokens] = (
+                        spread.astype(jnp.bfloat16)
+                    )
+
+    for i, (source, out) in enumerate(((h_ref, act_ref), (d_ref, grad_ref))):
+        rhs = source[...].reshape(slots * tokens, span)
+        for b in range(base_rows // lanes):
+            gram = jnp.dot(
+                lhs[i, b * mixed : (b + 1) * mixed], rhs, preferred_element_type=jnp.float32
             )
-            for q in range(span // 128):
-                mixed[q, pl.ds(s, block, slots), :] = gram[:, q * 128 : (q + 1) * 128] * scale
-        for q in range(span // 128):
-            lane = slice(n * span + q * 128, n * span + (q + 1) * 128)
-            out_ref[:, :, lane] = mixed[q].astype(jnp.bfloat16).reshape(block, slots, 128)
-
-
-def gram_call(block, gains, own_rows, normalized):
-    slots, tokens, width = block.shape
-    tile = min(128, own_rows)
-    out = pl.pallas_call(
-        functools.partial(gram_kernel, own_rows, 1.0 / tokens, normalized),
-        grid=(own_rows // tile,),
-        out_shape=jax.ShapeDtypeStruct((own_rows, slots, width), jnp.bfloat16),
-        in_specs=[
-            pl.BlockSpec(block.shape, lambda i: (0, 0, 0), pipeline_mode=pl.Buffered(1)),
-            pl.BlockSpec(gains.shape, lambda i: (0, 0, 0), pipeline_mode=pl.Buffered(1)),
+            out[b * lanes : (b + 1) * lanes] = (
+                (gram * scale).astype(jnp.bfloat16).reshape(lanes, slots, span)
+            )
+
+
+def gram_call(h_all, d_all, own_rows):
+    slots, tokens, width = h_all.shape
+    span = min(SPAN, width)
+    out = jax.ShapeDtypeStruct((own_rows, slots, width), jnp.bfloat16)
+    whole = pl.BlockSpec(memory_space=pl.ANY)
+    source = pl.BlockSpec((slots, tokens, span), lambda n: (0, 0, n))
+    target = pl.BlockSpec((own_rows, slots, span), lambda n: (0, 0, n))
+    outs = pl.pallas_call(
+        functools.partial(gram_kernel, own_rows, 1.0 / tokens),
+        grid=(width // span,),
+        out_shape=(out, out),
+        in_specs=[whole, whole, source, source],
+        out_specs=(target, target),
+        scratch_shapes=[
+            pltpu.VMEM((2, slots, tokens, own_rows), jnp.bfloat16),
+            pltpu.VMEM((2, own_rows * slots, slots * tokens), jnp.bfloat16),
+            pltpu.SemaphoreType.DMA((2,)),
         ],
-        out_specs=pl.BlockSpec((tile, slots, width), lambda i: (i, 0, 0)),
-        scratch_shapes=[
-            pltpu.VMEM((slots, tokens, width) if normalized else (slots, 8, 128), jnp.bfloat16),
-            pltpu.VMEM((4, tile * slots, 128), jnp.float32),
-        ],
-        compiler_params=pltpu.CompilerParams(vmem_limit_bytes=min(62 << 20, (32 << 20) + 8 * block.size)),
+        compiler_params=pltpu.CompilerParams(vmem_limit_bytes=60 << 20),
         name="gram",
-    )(block, gains)
-    return out.reshape(own_rows, slots, 1, width)
+    )(h_all, d_all, h_all, d_all)
+    return tuple(o.reshape(own_rows, slots, 1, width) for o in outs)
 
 
 def body(inputs, weights, norm_gains, cotangent):
@@ -800,8 +823,7 @@
     h_all, d_all = chain(inputs, weights, norm_gains, cotangent)
     h_all = h_all.reshape(slots, tokens, width)
     d_all = d_all.reshape(slots, tokens, width)
-    act = gram_call(h_all, norm_gains, own_rows, True)
-    return act, gram_call(d_all, norm_gains, own_rows, False)
+    return gram_call(h_all, d_all, own_rows)
 
 
 def solution(mesh):

time: 157 us -> 147 us (0.936)
  Pallas kernels: 154 us -> 147 us
  local copies, waits for them, and re-layouts: 2.34 us -> 0 us
    pallas_call x2 -> x1, Pallas kernels: 22.3 us -> 14.7 us  [gram_call(): pl.pallas_call(functools.partial(gram_kernel, own_rows, 1.0 / tokens), gr...]
    unnamed x6 -> x0, local copies, waits for them, and re-layouts: 2.34 us -> none
where the time goes in v4:
time: 147 us
  Pallas kernels  147 us (100%)
    pallas_call x1, Pallas kernels, chain(): pl.pallas_call(functools.partial(chain_kernel, dims), out_shape=(out, out...  132 us
    pallas_call x1, Pallas kernels, gram_call(): pl.pallas_call(functools.partial(gram_kernel, own_rows, 1.0 / tokens), gr...  14.7 us

profile of v4, /device:TPU:1, one launch (start us, length us, event | category | flops | bytes accessed | tf_op | source)
XLA Modules:
  0.0 147.3 jit_solution(2263700131342894203)
XLA Ops:
  0.6 131.9 %chain.1 = (bf16[2,2,4,32,4096]{4,3,2,1,0:T(8,128)(2,1)}, bf16[2,2,4,32,4096]{4,3,2,1,0:T(8,128)(2,1)}) custom-call(bf16[2,16,4096]{2,1,0:T(8,128)(2,1)} %x_ref.1, bf16[2,1,4096,1024]{3,2,1,0:T(8,128)(2,1)} %w_hbm.1, f32[2,1,4096]{2,1,0:T(1,128)} %g_ref.1, bf16[2,16,4096]{2,1,0:T(8,128)(2,1)} %cot_ref.1), custom_call_target="tpu_custom_call" | custom-call | tf_op jit(solution)/shard_map/chain/pallas_call | solution.py:688
  132.6 14.7 %gram.1 = (bf16[512,2,4096]{2,1,0:T(2,128)(2,1)}, bf16[512,2,4096]{2,1,0:T(2,128)(2,1)}) custom-call(bf16[2,256,4096]{2,1,0:T(8,128)(2,1)} %bitcast.8, bf16[2,256,4096]{2,1,0:T(8,128)(2,1)} %bitcast.10, bf16[2,256,4096]{2,1,0:T(8,128)(2,1)} %bitcast.9, bf16[2,256,4096]{2,1,0:T(8,128)(2,1)} %bitcast.11), custom_call_target="tpu_custom_call" | custom-call | tf_op jit(solution)/shard_map/gram/pallas_call | solution.py:798

commit v5 on v4

--- a/solution.py
+++ b/solution.py
@@ -10,6 +10,7 @@
 EPSILON = 1e-05
 SPLITS = 2
 CUTS = 1
+TALL = 128
 SPAN = 1024
 
 
@@ -224,7 +225,7 @@
         )
 
     def d_relays(item, slot, q):
-        for e, k in far_shares:
+        for e, k in reversed(far_shares):
             d_share(item, slot, q, e, k).wait_recv()
             d_relay(item, slot, q, e, k).start()
 
@@ -332,40 +333,51 @@
         inner = jnp.zeros((group, 1), jnp.float32)
         if not ahead:
             inverse_rms = rms[stored][:, :1]
-        order = [(3, r) for r in range(cuts)] + [(1, 0)] + [(2, r) for r in range(cuts)]
-        order += [(1, r) for r in range(1, cuts)] + [(0, r) for r in range(cuts)]
-        for k, r in order:
-            where_to = cut_ds(peer_of(c, k), r)
-            gain = g_ref[slot, :, where_to]
-            term = jnp.dot(columns, w_t[slot, :, where_to], preferred_element_type=jnp.float32)
-            if k == 3:
-                far_send[item, :, span(r)] = term.astype(jnp.bfloat16)
-                far_copy(item, r).start()
-            elif k == 1:
-                near_send[item, :, span(r)] = term.astype(jnp.bfloat16)
-                near_copy(item, r).start()
-            elif k == 2:
-                far_copy(item, r).wait_recv()
-                both = gain * (term + far_recv[item, :, span(r)].astype(jnp.float32))
+        terms = {}
+        for k in (3, 1, 2, 0):
+            for r in range(cuts):
+                where_to = cut_ds(peer_of(c, k), r)
+                term = matmul(columns, w_t[slot, :, where_to])
+                if k == 3:
+                    far_send[item, :, span(r)] = term.astype(jnp.bfloat16)
+                    far_copy(item, r).start()
+                elif k == 1:
+                    near_send[item, :, span(r)] = term.astype(jnp.bfloat16)
+                    near_copy(item, r).start()
+                else:
+                    terms[k, r] = term
                 if not ahead:
-                    both = inverse_rms * both
-                b_send[item, :, span(r)] = both.astype(jnp.bfloat16)
-                ab_copy(item, target_item, 2, r).start()
-            else:
-                near_copy(item, r).wait_recv()
-                both = gain * (term + near_recv[item, :, span(r)].astype(jnp.float32))
-                if not ahead:
-                    both = dcol[item, :, span(r)].astype(jnp.float32) + inverse_rms * both
-                a_send[item, :, span(r)] = both.astype(jnp.bfloat16)
-                ab_copy(item, target_item, 0, r).start()
+                    hidden = hbuf[stored, :, where_to].astype(jnp.float32)
+                    inner += jnp.sum(
+                        hidden * (g_ref[slot, :, where_to] * term), axis=-1, keepdims=True
+                    )
+        for r in range(cuts):
+            far_copy(item, r).wait_recv()
+            both = g_ref[slot, :, cut_ds(peer_of(c, 2), r)] * (
+                terms[2, r] + far_recv[item, :, span(r)].astype(jnp.float32)
+            )
             if not ahead:
-                hidden = hbuf[stored, :, where_to].astype(jnp.float32)
-                inner += jnp.sum(hidden * (gain * term), axis=-1, keepdims=True)
+                both = inverse_rms * both
+            b_send[item, :, span(r)] = both.astype(jnp.bfloat16)
+            ab_copy(item, target_item, 2, r).start()
         if not ahead:
             factor = inverse_rms * inverse_rms * inverse_rms * (inner * (1.0 / width))
             isend[item] = flat(factor, factor)
             for k in (2, 3, 0, 1):
                 inner_copy(item, target_item, k).start()
+        for r in range(cuts):
+            near_copy(item, r).wait_recv()
+            both = g_ref[slot, :, cut_ds(c, r)] * (
+                terms[0, r] + near_recv[item, :, span(r)].astype(jnp.float32)
+            )
+            if not ahead:
+                both = dcol[item, :, span(r)].astype(jnp.float32) + inverse_rms * both
+            a_send[item, :, span(r)] = both.astype(jnp.bfloat16)
+            ab_copy(item, target_item, 0, r).start()
+
+    def matmul(left, right):
+        tall = jnp.concatenate([left] * max(1, TALL // group), axis=0)
+        return jnp.dot(tall, right, preferred_element_type=jnp.float32)[:group]
 
     def turn_over(s):
         side = 256
@@ -413,7 +425,7 @@
         @pl.when(f_on & (layer > 0))
         def _():
             for r in range(cuts):
-                f_arrive(item, 0, r)
+                f_arrive(item, 2, r)
 
         @pl.when(f_on & (layer < layers - 1))
         def _():
@@ -424,48 +436,44 @@
 
             def piece(cc, r, first=False):
                 scaled, square = scaled_of(cc, r)
-                product = jnp.dot(
-                    scaled, w[slot, cut_ds(cc, r), :], preferred_element_type=jnp.float32
-                )
+                product = matmul(scaled, w[slot, cut_ds(cc, r), :])
                 if first:
                     acc[...] = product
                 else:
                     acc[...] += product
                 return square
 
-            total = piece(c, 0, True)
+            total = piece(peer_of(c, 2), 0, True)
             for r in range(1, cuts):
-                total += piece(c, r)
+                total += piece(peer_of(c, 2), r)
             for r in range(cuts):
 
                 @pl.when(layer > 0)
                 def _(r=r):
-                    f_arrive(item, 2, r)
-
-                total += piece(peer_of(c, 2), r)
+                    f_arrive(item, 0, r)
+
+                total += piece(c, r)
+            for r in range(cuts):
+
+                @pl.when(layer > 0)
+                def _(r=r):
+                    spread(item, 2, r, True).wait_recv()
+
+                total += piece(peer_of(c, 3), r)
             for r in range(cuts):
 
                 @pl.when(layer > 0)
                 def _(r=r):
                     spread(item, 0, r, True).wait_recv()
 
-                total += piece(peer_of(c, 1), r)
-            for r in range(cuts):
-
-                @pl.when(layer > 0)
-                def _(r=r):
-                    spread(item, 2, r, True).wait_recv()
-
                 if r < cuts - 1:
-                    total += piece(peer_of(c, 3), r)
-
-            last = cut_ds(peer_of(c, 3), cuts - 1)
-            scaled, square = scaled_of(peer_of(c, 3), cuts - 1)
+                    total += piece(peer_of(c, 1), r)
+
+            last = cut_ds(peer_of(c, 1), cuts - 1)
+            scaled, square = scaled_of(peer_of(c, 1), cuts - 1)
             inverse_rms = lax.rsqrt((total + square) * (1.0 / width) + EPSILON)
             for n in range(cuts):
-                product = acc[:, span(n)] + jnp.dot(
-                    scaled, w[slot, last, span(n)], preferred_element_type=jnp.float32
-                )
+                product = acc[:, span(n)] + matmul(scaled, w[slot, last, span(n)])
                 product = (product * inverse_rms).astype(jnp.bfloat16).astype(jnp.float32)
                 nxt[item, :, span(n)] = (
                     hbuf[item, :, cut_ds(c, n)].astype(jnp.float32) + product
@@ -494,7 +502,7 @@
         @pl.when(f_on & (layer == layers - 1))
         def _():
             for r in range(cuts):
-                f_arrive(item, 2, r)
+                f_arrive(item, 0, r)
             for r in range(cuts):
                 spread(item, 0, r, True).wait_recv()
                 spread(item, 2, r, True).wait_recv()

time: 147 us -> 143 us (0.973)
  Pallas kernels: 147 us -> 142 us
    pallas_call x1, Pallas kernels: 132 us -> 127 us  [chain(): pl.pallas_call(functools.partial(chain_kernel, dims), out_shape=(out, out...]
where the time goes in v5:
time: 143 us
  Pallas kernels  142 us (99%)
    pallas_call x1, Pallas kernels, chain(): pl.pallas_call(functools.partial(chain_kernel, dims), out_shape=(out, out...  127 us
    pallas_call x1, Pallas kernels, gram_call(): pl.pallas_call(functools.partial(gram_kernel, own_rows, 1.0 / tokens), gr...  14.7 us

profile of v5, /device:TPU:1, one launch (start us, length us, event | category | flops | bytes accessed | tf_op | source)
XLA Modules:
  0.0 142.8 jit_solution(15713832706363117429)
XLA Ops:
  0.6 127.5 %chain.1 = (bf16[2,2,4,32,4096]{4,3,2,1,0:T(8,128)(2,1)}, bf16[2,2,4,32,4096]{4,3,2,1,0:T(8,128)(2,1)}) custom-call(bf16[2,16,4096]{2,1,0:T(8,128)(2,1)} %x_ref.1, bf16[2,1,4096,1024]{3,2,1,0:T(8,128)(2,1)} %w_hbm.1, f32[2,1,4096]{2,1,0:T(1,128)} %g_ref.1, bf16[2,16,4096]{2,1,0:T(8,128)(2,1)} %cot_ref.1), custom_call_target="tpu_custom_call" | custom-call | tf_op jit(solution)/shard_map/chain/pallas_call | solution.py:696
  128.1 14.7 %gram.1 = (bf16[512,2,4096]{2,1,0:T(2,128)(2,1)}, bf16[512,2,4096]{2,1,0:T(2,128)(2,1)}) custom-call(bf16[2,256,4096]{2,1,0:T(8,128)(2,1)} %bitcast.8, bf16[2,256,4096]{2,1,0:T(8,128)(2,1)} %bitcast.10, bf16[2,256,4096]{2,1,0:T(8,128)(2,1)} %bitcast.9, bf16[2,256,4096]{2,1,0:T(8,128)(2,1)} %bitcast.11), custom_call_target="tpu_custom_call" | custom-call | tf_op jit(solution)/shard_map/gram/pallas_call | solution.py:806

commit v6 on v5

--- a/solution.py
+++ b/solution.py
@@ -100,8 +100,7 @@
     def w_copy(s):
         return pltpu.make_async_copy(w_hbm.at[s, 0], w.at[s], w_sem.at[s])
 
-    for s in range(slots):
-        w_copy(s).start()
+    w_copy(0).start()
 
     barrier = pltpu.get_barrier_semaphore()
     partners = [where(p, peer_of(c, k), d) for k in range(1, tensors)]
@@ -406,6 +405,12 @@
         def _():
             w_copy(slot).wait()
 
+        for s in range(1, slots):
+
+            @pl.when(t == (s - 1) * chunks)
+            def _(s=s):
+                w_copy(s).start()
+
         @pl.when(f_on & (q == 0) & (slot == slots - 1))
         def _():
             turn_over(slots - 1)
@@ -593,6 +598,10 @@
         def _():
             d_relays(item - 1, slot, q - 1)
 
+        @pl.when(b_on & (layer == 0) & (q > 1))
+        def _():
+            d_gather(item - 2, slot, q - 2)
+
         @pl.when(b_on & (slot > 0) & (layer < layers - 1) & (q == chunks - 1))
         def _():
             d_shares_all(item - (chunks - 1), slot)
@@ -610,7 +619,13 @@
                 d_relays(item, 0, q)
 
     for q in range(chunks):
-        d_gather((slots - 1) * chunks + q, 0, q)
+        if q >= chunks - 2:
+            d_gather((slots - 1) * chunks + q, 0, q)
+        else:
+
+            @pl.when(p > 0)
+            def _(q=q):
+                d_gather((slots - 1) * chunks + q, 0, q)
 
     @pl.when(p == 0)
     def _():

time: 143 us -> 143 us (level)
  no operation moved by 1% of the time
where the time goes in v6:
time: 143 us
  Pallas kernels  142 us (99%)
    pallas_call x1, Pallas kernels, chain(): pl.pallas_call(functools.partial(chain_kernel, dims), out_shape=(out, out...  127 us
    pallas_call x1, Pallas kernels, gram_call(): pl.pallas_call(functools.partial(gram_kernel, own_rows, 1.0 / tokens), gr...  14.7 us

profile of v6, /device:TPU:1, one launch (start us, length us, event | category | flops | bytes accessed | tf_op | source)
XLA Modules:
  0.0 142.8 jit_solution(16367612537994532317)
XLA Ops:
  0.6 127.4 %chain.1 = (bf16[2,2,4,32,4096]{4,3,2,1,0:T(8,128)(2,1)}, bf16[2,2,4,32,4096]{4,3,2,1,0:T(8,128)(2,1)}) custom-call(bf16[2,16,4096]{2,1,0:T(8,128)(2,1)} %x_ref.1, bf16[2,1,4096,1024]{3,2,1,0:T(8,128)(2,1)} %w_hbm.1, f32[2,1,4096]{2,1,0:T(1,128)} %g_ref.1, bf16[2,16,4096]{2,1,0:T(8,128)(2,1)} %cot_ref.1), custom_call_target="tpu_custom_call" | custom-call | tf_op jit(solution)/shard_map/chain/pallas_call | solution.py:711
  128.1 14.7 %gram.1 = (bf16[512,2,4096]{2,1,0:T(2,128)(2,1)}, bf16[512,2,4096]{2,1,0:T(2,128)(2,1)}) custom-call(bf16[2,256,4096]{2,1,0:T(8,128)(2,1)} %bitcast.8, bf16[2,256,4096]{2,1,0:T(8,128)(2,1)} %bitcast.10, bf16[2,256,4096]{2,1,0:T(8,128)(2,1)} %bitcast.9, bf16[2,256,4096]{2,1,0:T(8,128)(2,1)} %bitcast.11), custom_call_target="tpu_custom_call" | custom-call | tf_op jit(solution)/shard_map/gram/pallas_call | solution.py:821
